TPU v7x, 256 devices: a whole 4x4x8 slice. The times are simulated.
256 devices in a mesh: req: 64 (over z, x, core), tp: 4 (over y).
Axes of the slice: x: 4, y: 4, z: 8, core: 2. Of those that a mesh axis runs over, the one named last changes fastest.
Arguments:
- tokens_new: bfloat16 [64, 16, 2, 1024], P('req'), may hold values from -6 to 6
- prefix_len: int32 [64], replicated, may hold values from 1 to 4096, as said below
- tail_len: int32 [64, 16], P('req'), may hold values from 1 to 512, as said below
- pool_home: int32 [2048], replicated, may hold values from 0 to 63, as said below
- pool_page: int32 [2048], replicated, may hold values from 0 to 31
- slot_page_cache: bfloat16 [2048, 128, 2, 512], P('req', None, None, 'tp'), may hold values from -64 to 64
- tail_cache: bfloat16 [64, 16, 512, 2, 512], P('req', None, None, None, 'tp'), may hold values from -6 to 6
- routes: int32 [64, 16, 2, 8], P('req'), may hold values from 0 to 31, all different within a row; in each aligned block of 32 rows (0 to 31, 32 to 63, ..., all dimensions but the last counted through in order) at most 12 rows name the same one
- norm_gains: float32 [3, 1024], replicated, may hold values from 0.1 to 1.9
- query_weight: bfloat16 [1024, 1024], P(None, 'tp'), may hold values from -0.1875 to 0.1875
- key_value_weight: bfloat16 [1024, 2, 512], P(None, None, 'tp'), may hold values from -0.1875 to 0.1875
- out_weight: bfloat16 [1024, 1024], P('tp'), may hold values from -0.1875 to 0.1875
- router: bfloat16 [1024, 32], replicated, may hold values from -0.375 to 0.375
- expert_in: bfloat16 [64, 1024, 2, 512], P('req', None, None, 'tp'), as said below
- expert_out: bfloat16 [64, 512, 1024], P('req', 'tp'), as said below
- score_weight: float32 [1024], replicated, may hold values from -0.1875 to 0.1875
Outputs:
- layer_out: bfloat16 [64, 16, 2, 1024], P('req')
- row_score: float32 [64, 16, 2], P('req')
Inputs may be any that keep to these rules, and one draw needn't show every extreme that they name: `prefix_len`: some request has exactly 4096 prefix positions. `tail_len`: some sample has exactly 512 tail positions. `pool_home`: entry s * 32 + v describes slot v of the pool of device s of req. Every page 0 to 31 of every request lies in exactly one slot, and one device's pool holds either exactly 1 pages of a request or none of them. `routes`: in the 32 rows of one device no expert is named more than 12 times. `expert_in`: expert table copy c equals copy c mod 32. `expert_out`: expert table copy c equals copy c mod 32.
All inputs are finite; a program needn't handle non-finite values.
Results may differ from a plain program's by a relative error of at most 0.017.
Values may be sent and summed in bfloat16 or wider, within the bound.
A program may use at most 128 MiB of HBM per device.

v0:
```python
import jax
import jax.numpy as jnp
from jax import lax
from jax.sharding import PartitionSpec as P

HEAD_DIM = 64
MOST = 12


EPSILON = 1e-05
ROPE_BASE = 10000.0
LOWEST = -1e30


def rms_scale(values, gain_row):
    widened = values.astype(jnp.float32)
    return (
        widened
        * lax.rsqrt(jnp.mean(widened * widened, axis=-1, keepdims=True) + EPSILON)
        * gain_row
    )


def apply_rotary(vectors, token_positions):
    half_width = vectors.shape[-1] // 2
    frequency = ROPE_BASE ** (-jnp.arange(half_width, dtype=jnp.float32) / half_width)
    angles = token_positions.astype(jnp.float32)[..., None] * frequency
    cosine = jnp.cos(angles)[..., None, :]
    sine_part = jnp.sin(angles)[..., None, :]
    leading = vectors[..., :half_width]
    trailing = vectors[..., half_width:]
    return jnp.concatenate(
        [leading * cosine - trailing * sine_part, trailing * cosine + leading * sine_part], axis=-1
    )


def block_stats(scores, visible):
    block_top = jnp.max(jnp.where(visible, scores, LOWEST), axis=-1)
    weights = jnp.where(
        visible, jnp.exp(jnp.where(visible, scores - block_top[..., None], 0.0)), 0.0
    )
    return (block_top, jnp.sum(weights, axis=-1), weights.astype(jnp.bfloat16))


def shards(
    tokens_new,
    prefix_len,
    tail_len,
    pool_home,
    pool_page,
    slot_page_cache,
    tail_cache,
    routes,
    norm_gains,
    query_weight,
    key_value_weight,
    out_weight,
    router,
    expert_in,
    expert_out,
    score_weight,
):
    device = lax.axis_index("req")
    req_count = lax.axis_size("req")
    samples = tokens_new.shape[1]
    fresh_count = tokens_new.shape[2]
    model_width = tokens_new.shape[3]
    row_count = samples * fresh_count
    head_count = query_weight.shape[1] // HEAD_DIM
    kv_heads = key_value_weight.shape[2] // HEAD_DIM
    query_group_width = head_count // kv_heads
    pool_slots = slot_page_cache.shape[0]
    page_size = slot_page_cache.shape[1]
    slot_cap = max(1, pool_slots // req_count)
    score_scale = HEAD_DIM ** (-0.5)
    flat_tokens = tokens_new.reshape(row_count, model_width)
    normalized_input = rms_scale(flat_tokens, norm_gains[0]).astype(jnp.bfloat16)
    query_vectors = jnp.dot(
        normalized_input, query_weight, preferred_element_type=jnp.float32
    ).reshape(samples, fresh_count, head_count, HEAD_DIM)
    key_value_rows = jnp.dot(
        normalized_input,
        key_value_weight.reshape(model_width, 2 * kv_heads * HEAD_DIM),
        preferred_element_type=jnp.float32,
    ).reshape(samples, fresh_count, 2, kv_heads, HEAD_DIM)
    own_length = jnp.take(prefix_len, device)
    token_positions = (
        own_length + tail_len[0][:, None] + jnp.arange(fresh_count, dtype=jnp.int32)[None, :]
    )
    rotated_query = (
        apply_rotary(query_vectors, token_positions)
        .astype(jnp.bfloat16)
        .reshape(samples, fresh_count, kv_heads, query_group_width, HEAD_DIM)
    )
    key_rot = apply_rotary(key_value_rows[:, :, 0], token_positions).astype(jnp.bfloat16)
    value_new = key_value_rows[:, :, 1].astype(jnp.bfloat16)
    owner_homes = pool_home.reshape(req_count, pool_slots)
    owner_pages = pool_page.reshape(req_count, pool_slots)
    own_home = jnp.take(owner_homes, device, axis=0)
    slot_range = jnp.arange(pool_slots, dtype=jnp.int32)
    cap_range = jnp.arange(slot_cap, dtype=jnp.int32)
    same_home = own_home[:, None] == own_home[None, :]
    earlier = slot_range[:, None] <= slot_range[None, :]
    slot_rank = jnp.sum((same_home & earlier).astype(jnp.int32), axis=0)
    picked_slots = (
        own_home[None, None, :] == jnp.arange(req_count, dtype=jnp.int32)[:, None, None]
    ) & (slot_rank[None, None, :] == cap_range[None, :, None] + 1)
    slot_index = jnp.sum(
        picked_slots.astype(jnp.int32) * slot_range[None, None, :], axis=-1
    ).reshape(-1)
    page_range = jnp.arange(page_size, dtype=jnp.int32)
    outgoing = jnp.take(slot_page_cache, slot_index, axis=0).reshape(
        (req_count, slot_cap) + slot_page_cache.shape[1:]
    )
    arrived = lax.all_to_all(outgoing, "req", split_axis=0, concat_axis=0, tiled=True)
    home_match = owner_homes == device
    home_rank = jnp.cumsum(home_match.astype(jnp.int32), axis=1)
    wanted = home_match[:, None, :] & (home_rank[:, None, :] == cap_range[None, :, None] + 1)
    page_ids = jnp.where(
        jnp.any(wanted, axis=-1),
        jnp.sum(wanted.astype(jnp.int32) * owner_pages[:, None, :], axis=-1),
        -1,
    ).reshape(-1)
    blocks = arrived.reshape(req_count * slot_cap, page_size, 2, kv_heads, HEAD_DIM)
    page_scores = (
        jnp.einsum(
            "sikgd,btkd->bsikgt", rotated_query, blocks[:, :, 0], preferred_element_type=jnp.float32
        )
        * score_scale
    )
    page_spots = page_ids[:, None] * page_size + page_range[None, :]
    page_seen = ((page_spots < own_length) & (page_ids[:, None] >= 0))[:, None, None, None, None, :]
    page_top, page_total, page_weights = block_stats(page_scores, page_seen)
    page_numer = jnp.einsum(
        "bsikgt,btkd->bsikgd", page_weights, blocks[:, :, 1], preferred_element_type=jnp.float32
    )
    tail_count = tail_cache.shape[2]
    tail_block_list = tail_cache[0].reshape(
        samples, tail_count // page_size, page_size, 2, kv_heads, HEAD_DIM
    )
    tail_scores = (
        jnp.einsum(
            "sikgd,sbtkd->sbikgt",
            rotated_query,
            tail_block_list[:, :, :, 0],
            preferred_element_type=jnp.float32,
        )
        * score_scale
    )
    tail_spots = jnp.arange(tail_count, dtype=jnp.int32).reshape(tail_count // page_size, page_size)
    tail_seen = (tail_spots[None] < tail_len[0][:, None, None])[:, :, None, None, None, :]
    tail_top, tail_total, tail_weights = block_stats(tail_scores, tail_seen)
    tail_numer = jnp.einsum(
        "sbikgt,sbtkd->sbikgd",
        tail_weights,
        tail_block_list[:, :, :, 1],
        preferred_element_type=jnp.float32,
    )
    fresh_scores = (
        jnp.einsum("sikgd,sjkd->sikgj", rotated_query, key_rot, preferred_element_type=jnp.float32)
        * score_scale
    )
    fresh_range = jnp.arange(fresh_count, dtype=jnp.int32)
    fresh_seen = (fresh_range[None, :] <= fresh_range[:, None])[None, :, None, None, :]
    fresh_top, fresh_total, fresh_weights = block_stats(fresh_scores, fresh_seen)
    fresh_numer = jnp.einsum(
        "sikgj,sjkd->sikgd", fresh_weights, value_new, preferred_element_type=jnp.float32
    )
    overall = jnp.maximum(
        jnp.maximum(jnp.max(page_top, axis=0), jnp.max(tail_top, axis=1)), fresh_top
    )
    page_factor = jnp.exp(page_top - overall[None])
    tail_factor = jnp.exp(tail_top - overall[:, None])
    fresh_factor = jnp.exp(fresh_top - overall)
    denominator = (
        jnp.sum(page_factor * page_total, axis=0)
        + jnp.sum(tail_factor * tail_total, axis=1)
        + fresh_factor * fresh_total
    )
    numerator = (
        jnp.sum(page_factor[..., None] * page_numer, axis=0)
        + jnp.sum(tail_factor[..., None] * tail_numer, axis=1)
        + fresh_factor[..., None] * fresh_numer
    )
    attn_rows = (
        (numerator / denominator[..., None])
        .astype(jnp.bfloat16)
        .reshape(row_count, head_count * HEAD_DIM)
    )
    attn_part = jnp.dot(attn_rows, out_weight, preferred_element_type=jnp.float32)
    attn_out = lax.psum(attn_part, "tp")
    residual = (flat_tokens.astype(jnp.float32) + attn_out).astype(jnp.bfloat16)
    normed_moe = rms_scale(residual, norm_gains[1]).astype(jnp.bfloat16)
    logits = jnp.dot(normed_moe, router, preferred_element_type=jnp.float32)
    routing = routes.reshape(row_count, -1)
    top_count = routing.shape[1]
    expert_count = router.shape[1]
    expert_range = jnp.arange(expert_count, dtype=jnp.int32)
    route_table = (routing[:, :, None] == expert_range[None, None, :]).astype(jnp.float32)
    picked = jnp.sum(route_table * logits[:, None, :], axis=-1)
    gate_values = jax.nn.softmax(picked, axis=-1)
    local_experts = expert_in.shape[0]
    copies = local_experts * req_count // expert_count
    expert_slot = routing + expert_count * (device % copies)
    onehot = (routing.reshape(-1)[:, None] == expert_range[None, :]).astype(jnp.int32)
    arrival = jnp.sum(jnp.cumsum(onehot, axis=0) * onehot, axis=1) - 1
    target = (expert_slot.reshape(-1) * MOST + arrival).reshape(row_count, top_count)
    buffer = req_count * local_experts * MOST
    hits = (target[None, :, :] == jnp.arange(buffer, dtype=jnp.int32)[:, None, None]).astype(
        jnp.float32
    )
    spread = jnp.sum(hits, axis=-1).astype(jnp.bfloat16)
    combine = jnp.transpose(jnp.sum(hits * gate_values[None], axis=-1))
    outgoing_rows = (
        jnp.dot(spread, normed_moe, preferred_element_type=jnp.float32)
        .astype(jnp.bfloat16)
        .reshape(req_count, local_experts, MOST, model_width)
    )
    gate_up = jnp.einsum(
        "necd,edgf->necgf",
        lax.all_to_all(outgoing_rows, "req", split_axis=0, concat_axis=0, tiled=True),
        expert_in,
        preferred_element_type=jnp.float32,
    )
    hidden = (jax.nn.silu(gate_up[:, :, :, 0]) * gate_up[:, :, :, 1]).astype(jnp.bfloat16)
    result = jnp.einsum("necf,efd->necd", hidden, expert_out, preferred_element_type=jnp.float32)
    returned = lax.all_to_all(
        result.astype(jnp.bfloat16), "req", split_axis=0, concat_axis=0, tiled=True
    ).astype(result.dtype)
    mixed_part = jnp.dot(combine, returned.reshape(buffer, -1), precision=lax.Precision.HIGHEST)
    expert_mix = lax.psum(mixed_part.astype(jnp.bfloat16), "tp").astype(jnp.float32)
    layer_out = (residual.astype(jnp.float32) + expert_mix).astype(jnp.bfloat16)
    final_norm = rms_scale(layer_out, norm_gains[2])
    row_score = jnp.sum(final_norm * score_weight, axis=-1)
    return (
        layer_out.reshape(1, samples, fresh_count, model_width),
        row_score.reshape(1, samples, fresh_count),
    )


def solution(mesh):
    placed = (
        P("req", None, None, None),
        P(),
        P("req", None),
        P(),
        P(),
        P("req", None, None, "tp"),
        P("req", None, None, None, "tp"),
        P("req", None, None, None),
        P(),
        P(None, "tp"),
        P(None, None, "tp"),
        P("tp", None),
        P(),
        P("req", None, None, "tp"),
        P("req", "tp", None),
        P(),
    )
    return jax.shard_map(
        shards,
        mesh=mesh,
        in_specs=placed,
        out_specs=(P("req", None, None, None), P("req", None, None)),
        check_vma=False,
    )
```

profile of v0, /device:TPU:1, one launch (start us, length us, event | category | flops | bytes accessed | tf_op | source)
XLA Modules:
  0.0 398.5 jit_solution(14285597943707223789)
XLA Ops:
  7.2 0.9 reshape.516
  8.2 0.1 select_reduce_fusion.2
  8.4 0.4 copy-done
  8.8 10.7 %gather_fusion = bf16[64,128,2,128]{3,2,1,0:T(2,128)(2,1)} fusion(bf16[32,128,2,128]{3,2,1,0:T(2,128)(2,1)S(1)} %copy-done, s32[1024]{0:T(1024)S(1)} %pad_clamp_fusion), kind=kCustom, calls=%fused_computation | custom fusion | bytes 8388864 | tf_op jit(solution)/shard_map/jit(_take)/gather | solution.py:112
  19.4 7.9 %fusion.4 = bf16[64,1,128,2,128]{4,3,2,1,0:T(2,128)(2,1)} fusion(bf16[64,128,2,128]{3,2,1,0:T(2,128)(2,1)} %gather_fusion, pred[64]{0:T(512)(128)(4,1)S(1)} %compare_and_fusion), kind=kLoop, calls=%fused_computation.9 | loop fusion | flops 2097152 | bytes 8388672 | tf_op jit(solution)/shard_map/jit(_take)/select_n | solution.py:112
  27.4 13.3 %all-to-all-start = ((bf16[64,1,128,2,128]{4,3,2,1,0:T(2,128)(2,1)}), bf16[64,1,128,2,128]{4,3,2,1,0:T(2,128)(2,1)}, u32[]{:S(2)}, u32[]{:S(2)}) async-start(bf16[64,1,128,2,128]{4,3,2,1,0:T(2,128)(2,1)} %fusion.4), calls=%async_computation | async-start | bytes 8388608 | tf_op jit(solution)/shard_map/all_to_all | solution.py:115
  40.7 0.2 all-reduce.3.cloned.1.call-start
  41.2 0.6 dynamic-slice.5
  41.8 0.2 copy.276
  42.0 0.2 reduce_window_sum.26
  42.4 11.1 %copy.280 = bf16[1,16,512,2,128]{2,4,3,1,0:T(8,128)(2,1)} copy(bf16[1,16,512,2,128]{4,3,2,1,0:T(2,128)(2,1)} %param.22) | data formatting | bytes 8388608 | tf_op args[6]
  53.5 6.9 %reshape_squeeze.3 = bf16[16,4,128,2,2,64]{2,1,5,4,3,0:T(4,128)(2,1)} reshape(bf16[1,16,512,2,128]{2,4,3,1,0:T(8,128)(2,1)} %copy.280) | data formatting | bytes 8388608 | tf_op jit(solution)/shard_map/reshape;squeeze | solution.py:138
  61.2 0.1 multiply_reduce_fusion.2
  61.4 0.6 fusion.86
  62.0 0.1 multiply_cosine_fusion
  62.1 0.1 fusion.79
  62.3 0.3 fusion.47
  62.9 5.0 %fusion.85 = (bf16[16,4,128,1,2,64]{2,1,5,4,3,0:T(4,128)(2,1)S(1)}, bf16[16,4,128,1,2,64]{2,1,5,4,3,0:T(4,128)(2,1)}) fusion(bf16[16,4,128,2,2,64]{2,1,5,4,3,0:T(4,128)(2,1)} %reshape_squeeze.3), kind=kLoop, calls=%fused_computation.163 | loop fusion | bytes 8388608 | tf_op jit(solution)/shard_map/slice | solution.py:145
  68.0 0.6 fusion.31
  68.6 1.0 fusion.80
  69.6 0.7 copy.283
  70.3 0.2 copy.284
  70.6 0.3 fusion.45
  71.2 0.7 fusion.58
  71.8 0.2 copy.288
  72.1 0.7 fusion.83
  72.8 0.1 copy.304
  72.9 0.6 reduce-window.6
  73.5 0.2 slice_reduce_fusion
  74.0 0.1 select_reduce_fusion.3
  74.1 0.1 reduce_or.9
  74.3 0.2 fusion.65
  74.5 60.6 %all-to-all-done = bf16[64,1,128,2,128]{4,3,2,1,0:T(2,128)(2,1)} async-done(((bf16[64,1,128,2,128]{4,3,2,1,0:T(2,128)(2,1)}), bf16[64,1,128,2,128]{4,3,2,1,0:T(2,128)(2,1)}, u32[]{:S(2)}, u32[]{:S(2)}) %all-to-all-start) | async-done | bytes 4194336 | tf_op jit(solution)/shard_map/all_to_all | solution.py:115
  135.1 10.9 %copy.272 = bf16[64,1,128,2,128]{2,4,3,0,1:T(8,128)(2,1)} copy(bf16[64,1,128,2,128]{4,3,2,1,0:T(2,128)(2,1)} %all-to-all-done) | data formatting | bytes 8388608 | tf_op jit(solution)/shard_map/all_to_all | solution.py:115
  146.0 3.1 fusion.6
  149.1 3.3 fusion.7
  152.5 0.3 multiply_reduce_fusion
  152.8 0.2 multiply_reduce_fusion.1
  153.1 0.7 fusion.72
  153.8 11.1 %copy.345 = bf16[64,1,128,2,128]{2,4,0,3,1:T(8,128)(2,1)} copy(bf16[64,1,128,2,128]{4,3,2,1,0:T(2,128)(2,1)} %all-to-all-done) | data formatting | bytes 8388608 | tf_op jit(solution)/shard_map/reshape | solution.py:124
  164.9 3.0 fusion
  167.9 1.3 fusion.24
  169.2 0.1 fusion.44
  169.5 0.9 fusion.87
  170.3 0.3 all-reduce.5.cloned.1.call-start
  170.6 42.1 %all-reduce.3.cloned.1.call-done = f32[32,1024]{1,0:T(8,128)} async-done(((f32[32,1024]{1,0:T(8,128)}), f32[32,1024]{1,0:T(8,128)}) %all-reduce.3.cloned.1.call-update) | async-done | bytes 131088 | tf_op jit(solution)/shard_map/psum | solution.py:191
  212.7 1.0 fusion.37
  213.7 0.2 fusion.61
  213.9 0.2 select_reduce_fusion.1
  214.4 0.6 convert_reduce_fusion
  215.0 1.8 convolution_convert_fusion
  216.8 2.4 reshape.522
  219.2 62.3 %all_to_all.15 = bf16[64,1,12,1024]{3,2,1,0:T(8,128)(2,1)S(1)} all-to-all(bf16[64,1,12,1024]{3,2,1,0:T(8,128)(2,1)S(1)} %bitcast.214), channel_id=1, replica_groups=mesh['req'=64,'tp'=4] {'req'}, dimensions={0} | all-to-all | bytes 3145728 | tf_op jit(solution)/shard_map/all_to_all | solution.py:221
  281.6 1.8 fusion.17
  283.4 0.6 fusion.16
  284.0 0.9 copy.321
  284.9 56.7 %all_to_all.16 = bf16[64,1,12,1024]{3,2,1,0:T(8,128)(2,1)} all-to-all(bf16[64,1,12,1024]{3,2,1,0:T(8,128)(2,1)S(1)} %copy.321), channel_id=1, replica_groups=mesh['req'=64,'tp'=4] {'req'}, dimensions={0} | all-to-all | bytes 3145728 | tf_op jit(solution)/shard_map/all_to_all | solution.py:227
  341.6 3.6 reshape.526
  345.2 2.9 convolution_convert_fusion.2
  348.2 40.9 %all-reduce.5.cloned.1.call-done = bf16[32,1024]{1,0:T(8,128)(2,1)} async-done(((bf16[32,1024]{1,0:T(8,128)(2,1)}), bf16[32,1024]{1,0:T(8,128)(2,1)}) %all-reduce.5.cloned.1.call-update) | async-done | bytes 65552 | tf_op jit(solution)/shard_map/psum | solution.py:231
  389.1 1.0 fusion.33
  390.1 0.7 reshape.527
  390.7 0.2 fusion.36
  391.0 0.7 copy.322
  (93 shorter events, 2.6 us)
Async XLA Ops:
  7.2 1.6 copy-start
  27.3 13.6 %copy-start.12 = (s32[1,16,2,8]{1,3,2,0:T(8,128)S(1)}, s32[1,16,2,8]{1,3,2,0:T(8,128)}, u32[]{:S(2)}) copy-start(s32[1,16,2,8]{1,3,2,0:T(8,128)} %param.23) | copy-start | bytes 3076
  27.3 13.9 %copy-start.18 = (s32[64]{0:T(128)S(1)}, s32[64]{0:T(128)}, u32[]{:S(2)}) copy-start(s32[64]{0:T(128)} %param.17) | copy-start | bytes 772
  27.3 14.5 %copy-start.4 = (bf16[1024,256]{1,0:T(8,128)(2,1)S(1)}, bf16[1024,256]{1,0:T(8,128)(2,1)}, u32[]{:S(2)}) copy-start(bf16[1024,256]{1,0:T(8,128)(2,1)} %param.25) | copy-start | bytes 1572868
  27.3 14.9 %copy-start.8 = (s32[2048]{0:T(1024)S(1)}, s32[2048]{0:T(1024)}, u32[]{:S(2)}) copy-start(s32[2048]{0:T(1024)} %param.19) | copy-start | bytes 24580
  27.3 15.0 %copy-start.13 = (s32[2048]{0:T(1024)S(1)}, s32[2048]{0:T(1024)}, u32[]{:S(2)}) copy-start(s32[2048]{0:T(1024)} %param.20) | copy-start | bytes 24580
  27.4 107.7 %all-to-all-start = ((bf16[64,1,128,2,128]{4,3,2,1,0:T(2,128)(2,1)}), bf16[64,1,128,2,128]{4,3,2,1,0:T(2,128)(2,1)}, u32[]{:S(2)}, u32[]{:S(2)}) async-start(bf16[64,1,128,2,128]{4,3,2,1,0:T(2,128)(2,1)} %fusion.4), calls=%async_computation | async-start | bytes 8388608 | tf_op jit(solution)/shard_map/all_to_all | solution.py:115
  40.7 172.0 %all-reduce.3.cloned.1.call-start = ((), (), s32[]{:S(2)}) async-start(), calls=%async_computation.3 | async-start | bytes 262144 | tf_op jit(solution)/shard_map/psum | solution.py:191
  53.5 7.0 %copy-start.3 = (bf16[1,16,2,1024]{3,2,1,0:T(2,128)(2,1)S(1)}, bf16[1,16,2,1024]{3,2,1,0:T(2,128)(2,1)}, u32[]{:S(2)}) copy-start(bf16[1,16,2,1024]{3,2,1,0:T(2,128)(2,1)} %param.16) | copy-start | bytes 196612
  53.5 7.8 %copy-start.15 = (s32[1,16]{1,0:T(1,128)S(1)}, s32[1,16]{1,0:T(1,128)}, u32[]{:S(2)}) copy-start(s32[1,16]{1,0:T(1,128)} %param.18) | copy-start | bytes 196
  53.5 7.8 %copy-start.11 = (f32[3,1024]{1,0:T(4,128)S(1)}, f32[3,1024]{1,0:T(4,128)}, u32[]{:S(2)}) copy-start(f32[3,1024]{1,0:T(4,128)} %param.24) | copy-start | bytes 36868
  68.0 2.3 copy-start.5
  149.1 3.3 copy-start.10
  164.9 3.0 copy-start.2
  167.9 1.6 copy-start.6
  167.9 45.8 %copy-start.17 = (bf16[1024,32]{0,1:T(8,128)(2,1)S(1)}, bf16[1024,32]{0,1:T(8,128)(2,1)}, u32[]{:S(2)}) copy-start(bf16[1024,32]{0,1:T(8,128)(2,1)} %param.28) | copy-start | bytes 196612
  170.3 218.7 %all-reduce.5.cloned.1.call-start = ((), (), s32[]{:S(2)}) async-start(), calls=%async_computation.4 | async-start | bytes 131072 | tf_op jit(solution)/shard_map/psum | solution.py:231
  216.8 64.8 %copy-start.16 = (bf16[1,1024,2,128]{3,2,1,0:T(2,128)(2,1)S(1)}, bf16[1,1024,2,128]{3,2,1,0:T(2,128)(2,1)}, u32[]{:S(2)}) copy-start(bf16[1,1024,2,128]{3,2,1,0:T(2,128)(2,1)} %param.29) | copy-start | bytes 1572868
  219.2 64.1 %copy-start.7 = (bf16[1,128,1024]{2,1,0:T(8,128)(2,1)S(1)}, bf16[1,128,1024]{2,1,0:T(8,128)(2,1)}, u32[]{:S(2)}) copy-start(bf16[1,128,1024]{2,1,0:T(8,128)(2,1)} %param.30) | copy-start | bytes 786436
  284.9 106.8 %copy-start.1 = (bf16[32,128,2,128]{3,2,1,0:T(2,128)(2,1)S(1)}, bf16[32,128,2,128]{3,2,1,0:T(2,128)(2,1)}, u32[]{:S(2)}) copy-start(bf16[32,128,2,128]{3,2,1,0:T(2,128)(2,1)} %param.21) | copy-start | bytes 6291460
  341.6 49.1 %copy-start.9 = (f32[1,1024]{1,0:T(1,128)S(1)}, f32[1,1024]{1,0:T(1,128)}, u32[]{:S(2)}) copy-start(f32[1,1024]{1,0:T(1,128)} %get-tuple-element.70) | copy-start | bytes 12292
  341.6 49.1 %copy-start.14 = (f32[1024]{0:T(1024)S(1)}, f32[1024]{0:T(1024)}, u32[]{:S(2)}) copy-start(f32[1024]{0:T(1024)} %param.31) | copy-start | bytes 12292
Sparse Core Ops, SparseCore 0:
  170.5 42.1 all-reduce.2
  348.3 40.7 all-reduce.4
where the time goes:
time: 401 us; the launch traced here: 399 us
  waiting for transfers between devices  144 us (36%)
  blocking collectives  119 us (30%)
  local copies, waits for them, and re-layouts  69.5 us (17%)
  other arithmetic  19.8 us (5%)
  matrix products  17.5 us (4%)
  between operations  15.2 us (4%)
  starting transfers between devices  13.8 us (3%)
    all_to_all x1, blocking collectives, shards(): lax.all_to_all(outgoing_rows, 'req', split_axis=0, concat_axis=0, tiled=T...  62.3 us
    all_to_all x1, waiting for transfers between devices, shards(): lax.all_to_all(outgoing, 'req', split_axis=0, concat_axis=0, tiled=True)  60.6 us
    all_to_all x1, blocking collectives, shards(): lax.all_to_all(result.astype(jnp.bfloat16), 'req', split_axis=0, concat_a...  56.7 us
    psum x1, waiting for transfers between devices, shards(): attn_out = lax.psum(attn_part, 'tp')  42.1 us
    psum x1, waiting for transfers between devices, shards(): lax.psum(mixed_part.astype(jnp.bfloat16), 'tp').astype(jnp.float32)  40.9 us
    all_to_all x1, starting transfers between devices, shards(): lax.all_to_all(outgoing, 'req', split_axis=0, concat_axis=0, tiled=True)  13.3 us
    unnamed x43, local copies, waits for them, and re-layouts  12.7 us
    reshape x1, local copies, waits for them, and re-layouts, shards(): arrived.reshape(req_count * slot_cap, page_size, 2, kv_heads, HEAD_DIM)  11.1 us
  transfers between devices with their start and end apart: 3, of which 3 were waited for; matrix products, arithmetic and copies ran while one was open for 8% of the time, Pallas kernels for 0%

commit v1 on v0

--- a/solution.py
+++ b/solution.py
@@ -1,6 +1,8 @@
 import jax
 import jax.numpy as jnp
 from jax import lax
+from jax.experimental import pallas as pl
+from jax.experimental.pallas import tpu as pltpu
 from jax.sharding import PartitionSpec as P
 
 HEAD_DIM = 64
@@ -40,6 +42,297 @@
         visible, jnp.exp(jnp.where(visible, scores - block_top[..., None], 0.0)), 0.0
     )
     return (block_top, jnp.sum(weights, axis=-1), weights.astype(jnp.bfloat16))
+
+
+MESH = pl.DeviceIdType.MESH
+F32 = jnp.float32
+BF16 = jnp.bfloat16
+
+
+def iota(shape, dim):
+    return lax.broadcasted_iota(jnp.int32, shape, dim)
+
+
+def mm(a, b):
+    return lax.dot_general(a, b, (((1,), (0,)), ((), ())), preferred_element_type=F32)
+
+
+def mm_t(a, b):
+    return lax.dot_general(a, b, (((1,), (1,)), ((), ())), preferred_element_type=F32)
+
+
+def remote(src, dst, send_sem, recv_sem, req, tp):
+    return pltpu.make_async_remote_copy(
+        src_ref=src,
+        dst_ref=dst,
+        send_sem=send_sem,
+        recv_sem=recv_sem,
+        device_id=(req, tp),
+        device_id_type=MESH,
+    )
+
+
+def spread_halves(values):
+    high = values.astype(BF16)
+    return high, (values - high.astype(F32)).astype(BF16)
+
+
+def deinterleave(src_ref, dst_ref):
+    row = iota((256, 256), 0)
+    pick = (iota((256, 256), 1) == 2 * (row % 128) + row // 128).astype(BF16)
+    for block in range(src_ref.shape[0] // 256):
+        both = mm(pick, src_ref[pl.ds(block * 256, 256), :]).astype(BF16)
+        dst_ref[pl.ds(block * 128, 128), 0:128] = both[:128]
+        dst_ref[pl.ds(block * 128, 128), 128:256] = both[128:]
+
+
+def rms(values, gain):
+    return values * lax.rsqrt(jnp.mean(values * values, axis=-1, keepdims=True) + EPSILON) * gain
+
+
+def exchange_start(slots, send_sem, recv_sem, req, tp):
+    for step in (1, 3, 2):
+        remote(
+            slots.at[tp], slots.at[tp], send_sem.at[step], recv_sem.at[tp], req, (tp + step) % 4
+        ).start()
+
+
+def exchange_finish(slots, send_sem, recv_sem, req, tp):
+    for step in (1, 3, 2):
+        other = (tp + step) % 4
+        copy = remote(slots.at[tp], slots.at[other], send_sem.at[step], recv_sem.at[other], req, other)
+        copy.wait_recv()
+    for step in (1, 3, 2):
+        copy = remote(slots.at[tp], slots.at[tp], send_sem.at[step], recv_sem.at[tp], req, tp)
+        copy.wait_send()
+    return (
+        slots[0].astype(F32) + slots[1].astype(F32) + slots[2].astype(F32) + slots[3].astype(F32)
+    )
+
+
+def route_tables(routes):
+    column = iota((32, 32), 1)
+    uses = jnp.zeros((32, 32), F32)
+    for k in range(8):
+        uses = uses + (routes[:, k : k + 1] == column).astype(F32)
+    earlier = (iota((32, 32), 0) > column).astype(BF16)
+    rank = mm(earlier, uses.astype(BF16))
+    return uses, jnp.where(uses > 0, rank, -1.0).astype(BF16)
+
+
+def spread_matrices(rank):
+    repeat = (iota((256, 32), 0) // 8 == iota((256, 32), 1)).astype(BF16)
+    slot = (iota((256, 32), 0) % 8).astype(F32)
+    whole = (mm_t(repeat, rank) == slot).astype(F32).astype(BF16)
+    slot2 = iota((256, 64), 0) % 8
+    at_half = mm_t(repeat, jnp.concatenate([rank, rank], axis=0))
+    half = (
+        jnp.where(iota((256, 64), 1) // 32 == slot2 // 4, at_half, -1.0)
+        == (8 + slot2 % 4).astype(F32)
+    )
+    return whole, half.astype(F32).astype(BF16)
+
+
+def combine_matrices(rank, gates):
+    repeat = (iota((256, 32), 0) // 8 == iota((256, 32), 1)).astype(BF16)
+    at = mm_t(rank, repeat)
+    gate_parts = [mm_t(part, repeat) for part in spread_halves(gates)]
+    slot = iota((32, 256), 1) % 8
+    chosen = [at == slot.astype(F32)]
+    for h in range(2):
+        chosen.append(jnp.where(slot // 4 == h, at, -1.0) == (8 + slot % 4).astype(F32))
+    return [[jnp.where(pick, part, 0.0).astype(BF16) for part in gate_parts] for pick in chosen]
+
+
+def moe_stage(req, tp, residual, routes_ref, gains_ref, router_ref, eout_ref, score_ref,
+              out_ref, row_score_ref, win, out_buf, in_buf, ret_buf, back_buf, mix_slots,
+              dsend, drecv, rsend, rrecv, lsem, msend, mrecv):
+    z = req // 8
+    xc = req % 8
+    core = req % 2
+    far = jnp.where(core == 0, 2, 6)
+    hops = (0, 1, 7, far)
+
+    uses, rank = route_tables(routes_ref[...])
+    whole, half = spread_matrices(rank)
+    normed = rms(residual.astype(F32), gains_ref[1:2, :]).astype(BF16)
+    out_buf[:, :, 0:1024] = mm(whole, normed).reshape(32, 8, 1024).astype(BF16)
+    stacked = jnp.concatenate([normed[:, :512], normed[:, 512:]], axis=0)
+    out_buf[:, :, 1024:1536] = mm(half, stacked).reshape(32, 8, 512).astype(BF16)
+
+    for g in (3, 2, 1, 0):
+        to_z = (z + hops[g]) % 8
+        base = (to_z % 4) * 8
+
+        @pl.loop(1, 8)
+        def _(i):
+            other = (xc + i) % 8
+            remote(
+                out_buf.at[base + other], in_buf.at[g, xc], dsend.at[g, i], drecv.at[g, xc],
+                to_z * 8 + other, tp,
+            ).start()
+
+        if g == 0:
+            pltpu.make_async_copy(out_buf.at[base + xc], in_buf.at[0, xc], lsem.at[0]).start()
+        else:
+            remote(
+                out_buf.at[base + xc], in_buf.at[g, xc], dsend.at[g, 0], drecv.at[g, xc],
+                to_z * 8 + xc, tp,
+            ).start()
+
+    logits = mm_t(normed, router_ref[...])
+    shown = jnp.where(uses > 0, logits, LOWEST)
+    weights = jnp.where(uses > 0, jnp.exp(shown - jnp.max(shown, axis=-1, keepdims=True)), 0.0)
+    gates = weights / jnp.sum(weights, axis=-1, keepdims=True)
+    combine = combine_matrices(rank, gates)
+
+    own_expert = (z % 4) * 8 + xc
+    backs = (0, 7, 1, (8 - far) % 8)
+    upper = iota((64, 1), 0) % 8 < 4
+
+    for g in range(4):
+        def from_z(other):
+            if g < 3:
+                return (z + backs[g]) % 8
+            return (z + jnp.where(other % 2 == 0, 6, 2)) % 8
+
+        if g == 0:
+            pltpu.make_async_copy(out_buf.at[own_expert], in_buf.at[0, xc], lsem.at[0]).wait()
+
+        @pl.loop(1 if g == 0 else 0, 8)
+        def _(i):
+            other = (xc + i) % 8
+            remote(
+                out_buf.at[0], in_buf.at[g, other], dsend.at[g, i], drecv.at[g, other], req, tp
+            ).wait_recv()
+
+        rows = in_buf[g].astype(F32)
+        rows_a = rows[:, :, :1024].reshape(64, 1024).astype(BF16)
+        rows_b = rows[:, :, 1024:].reshape(64, 512).astype(BF16)
+        up_a = mm(rows_a, win[...])
+        low = mm(rows_b, win[0:512, :])
+        high = mm(rows_b, win[512:1024, :])
+        mine = jnp.where(upper, low, high)
+        swapped = jnp.where(upper, pltpu.roll(mine, 60, 0), pltpu.roll(mine, 4, 0))
+        up_b = mine + swapped
+        both = jnp.concatenate([up_a, up_b], axis=0)
+        gate = both[:, :128]
+        hidden = (gate / (1.0 + jnp.exp(-gate)) * both[:, 128:]).astype(BF16)
+        result = mm(hidden, eout_ref[...])
+        ret_buf[g, :, :, 0:1024] = result[:64].reshape(8, 8, 1024).astype(BF16)
+        second = result[64:]
+        ret_buf[g, :, :, 1024:1536] = (
+            jnp.where(upper, second[:, :512], second[:, 512:]).reshape(8, 8, 512).astype(BF16)
+        )
+
+        if g == 0:
+            pltpu.make_async_copy(ret_buf.at[0, xc], back_buf.at[own_expert], lsem.at[1]).start()
+
+        @pl.loop(1 if g == 0 else 0, 8)
+        def _(i):
+            other = (xc + i) % 8
+            remote(
+                ret_buf.at[g, other], back_buf.at[own_expert], rsend.at[g, i],
+                rrecv.at[own_expert], from_z(other) * 8 + other, tp,
+            ).start()
+
+    pltpu.make_async_copy(ret_buf.at[0, xc], back_buf.at[own_expert], lsem.at[1]).wait()
+
+    @pl.loop(1, 32)
+    def _(i):
+        expert = (own_expert + i) % 32
+        remote(
+            ret_buf.at[0, 0], back_buf.at[expert], rsend.at[0, 0], rrecv.at[expert], req, tp
+        ).wait_recv()
+
+    back = back_buf[...].astype(F32)
+    back_a = back[:, :, :1024].reshape(256, 1024).astype(BF16)
+    back_b = back[:, :, 1024:].reshape(256, 512).astype(BF16)
+    mix_b = [mm(combine[1 + h][0], back_b) + mm(combine[1 + h][1], back_b) for h in range(2)]
+    mix = mm(combine[0][0], back_a) + mm(combine[0][1], back_a)
+    mix = mix + jnp.concatenate(mix_b, axis=1)
+    mix_slots[tp] = mix.astype(BF16)
+    exchange_start(mix_slots, msend, mrecv, req, tp)
+
+    for g in range(4):
+
+        @pl.loop(1 if g == 0 else 0, 8)
+        def _(i):
+            remote(
+                out_buf.at[0], in_buf.at[g, 0], dsend.at[g, i], drecv.at[g, 0], req, tp
+            ).wait_send()
+            remote(
+                ret_buf.at[g, 0], back_buf.at[0], rsend.at[g, i], rrecv.at[0], req, tp
+            ).wait_send()
+
+    expert_mix = exchange_finish(mix_slots, msend, mrecv, req, tp)
+    layer_out = (residual.astype(F32) + expert_mix).astype(BF16)
+    out_ref[...] = layer_out
+    final = rms(layer_out.astype(F32), gains_ref[2:3, :])
+    row_score_ref[...] = jnp.sum(final * score_ref[...], axis=-1, keepdims=True)
+
+
+def moe_scratch():
+    dma = pltpu.SemaphoreType.DMA
+    return [
+        pltpu.VMEM((1024, 256), BF16),
+        pltpu.VMEM((32, 8, 1536), BF16),
+        pltpu.VMEM((4, 8, 8, 1536), BF16),
+        pltpu.VMEM((4, 8, 8, 1536), BF16),
+        pltpu.VMEM((32, 8, 1536), BF16),
+        pltpu.VMEM((4, 32, 1024), BF16),
+        dma((4, 8)),
+        dma((4, 8)),
+        dma((4, 8)),
+        dma((32,)),
+        dma((2,)),
+        dma((4,)),
+        dma((4,)),
+    ]
+
+
+def moe_kernel(tok_ref, part_ref, routes_ref, gains_ref, router_ref, ein_ref, eout_ref, score_ref,
+               out_ref, row_score_ref, attn_slots, asend, arecv, win, *rest):
+    req = lax.axis_index("req")
+    tp = lax.axis_index("tp")
+    z = req // 8
+    xc = req % 8
+    barrier = pltpu.get_barrier_semaphore()
+    for step in (1, 2, 3):
+        pl.semaphore_signal(barrier, 1, device_id=(req, (tp + step) % 4), device_id_type=MESH)
+
+    @pl.loop(1, 40)
+    def _(i):
+        other = ((z + 6 + (i // 8 + 2) % 5) % 8) * 8 + (xc + i) % 8
+        pl.semaphore_signal(barrier, 1, device_id=(other, tp), device_id_type=MESH)
+
+    attn_slots[tp] = part_ref[...].astype(BF16)
+    pl.semaphore_wait(barrier, 42)
+    exchange_start(attn_slots, asend, arecv, req, tp)
+    deinterleave(ein_ref, win)
+    attn_out = exchange_finish(attn_slots, asend, arecv, req, tp)
+    residual = (tok_ref[...].astype(F32) + attn_out).astype(BF16)
+    moe_stage(req, tp, residual, routes_ref, gains_ref, router_ref, eout_ref, score_ref,
+              out_ref, row_score_ref, win, *rest)
+
+
+def moe_call(flat_tokens, attn_part, routing, norm_gains, router, expert_in, expert_out, score_weight):
+    dma = pltpu.SemaphoreType.DMA
+    vmem = pl.BlockSpec(memory_space=pltpu.VMEM)
+    return pl.pallas_call(
+        moe_kernel,
+        out_shape=(
+            jax.ShapeDtypeStruct((32, 1024), BF16),
+            jax.ShapeDtypeStruct((32, 1), F32),
+        ),
+        in_specs=[vmem] * 8,
+        out_specs=(vmem, vmem),
+        scratch_shapes=[pltpu.VMEM((4, 32, 1024), BF16), dma((4,)), dma((4,))] + moe_scratch(),
+        compiler_params=pltpu.CompilerParams(
+            collective_id=0, has_side_effects=True, vmem_limit_bytes=48 * 1024 * 1024
+        ),
+    )(flat_tokens, attn_part, routing, norm_gains, router.T, expert_in.reshape(2048, 128),
+      expert_out[0], score_weight[None])
 
 
 def shards(
@@ -188,50 +481,10 @@
         .reshape(row_count, head_count * HEAD_DIM)
     )
     attn_part = jnp.dot(attn_rows, out_weight, preferred_element_type=jnp.float32)
-    attn_out = lax.psum(attn_part, "tp")
-    residual = (flat_tokens.astype(jnp.float32) + attn_out).astype(jnp.bfloat16)
-    normed_moe = rms_scale(residual, norm_gains[1]).astype(jnp.bfloat16)
-    logits = jnp.dot(normed_moe, router, preferred_element_type=jnp.float32)
-    routing = routes.reshape(row_count, -1)
-    top_count = routing.shape[1]
-    expert_count = router.shape[1]
-    expert_range = jnp.arange(expert_count, dtype=jnp.int32)
-    route_table = (routing[:, :, None] == expert_range[None, None, :]).astype(jnp.float32)
-    picked = jnp.sum(route_table * logits[:, None, :], axis=-1)
-    gate_values = jax.nn.softmax(picked, axis=-1)
-    local_experts = expert_in.shape[0]
-    copies = local_experts * req_count // expert_count
-    expert_slot = routing + expert_count * (device % copies)
-    onehot = (routing.reshape(-1)[:, None] == expert_range[None, :]).astype(jnp.int32)
-    arrival = jnp.sum(jnp.cumsum(onehot, axis=0) * onehot, axis=1) - 1
-    target = (expert_slot.reshape(-1) * MOST + arrival).reshape(row_count, top_count)
-    buffer = req_count * local_experts * MOST
-    hits = (target[None, :, :] == jnp.arange(buffer, dtype=jnp.int32)[:, None, None]).astype(
-        jnp.float32
-    )
-    spread = jnp.sum(hits, axis=-1).astype(jnp.bfloat16)
-    combine = jnp.transpose(jnp.sum(hits * gate_values[None], axis=-1))
-    outgoing_rows = (
-        jnp.dot(spread, normed_moe, preferred_element_type=jnp.float32)
-        .astype(jnp.bfloat16)
-        .reshape(req_count, local_experts, MOST, model_width)
-    )
-    gate_up = jnp.einsum(
-        "necd,edgf->necgf",
-        lax.all_to_all(outgoing_rows, "req", split_axis=0, concat_axis=0, tiled=True),
-        expert_in,
-        preferred_element_type=jnp.float32,
-    )
-    hidden = (jax.nn.silu(gate_up[:, :, :, 0]) * gate_up[:, :, :, 1]).astype(jnp.bfloat16)
-    result = jnp.einsum("necf,efd->necd", hidden, expert_out, preferred_element_type=jnp.float32)
-    returned = lax.all_to_all(
-        result.astype(jnp.bfloat16), "req", split_axis=0, concat_axis=0, tiled=True
-    ).astype(result.dtype)
-    mixed_part = jnp.dot(combine, returned.reshape(buffer, -1), precision=lax.Precision.HIGHEST)
-    expert_mix = lax.psum(mixed_part.astype(jnp.bfloat16), "tp").astype(jnp.float32)
-    layer_out = (residual.astype(jnp.float32) + expert_mix).astype(jnp.bfloat16)
-    final_norm = rms_scale(layer_out, norm_gains[2])
-    row_score = jnp.sum(final_norm * score_weight, axis=-1)
+    layer_out, row_score = moe_call(
+        flat_tokens, attn_part, routes.reshape(row_count, -1), norm_gains, router, expert_in,
+        expert_out, score_weight,
+    )
     return (
         layer_out.reshape(1, samples, fresh_count, model_width),
         row_score.reshape(1, samples, fresh_count),

time: 401 us -> 214 us (0.53)
  blocking collectives: 119 us -> 0 us
  waiting for transfers between devices: 144 us -> 57.9 us
  Pallas kernels: 0 us -> 45.2 us
  between operations: 15.2 us -> 1.7 us
  local copies, waits for them, and re-layouts: 69.5 us -> 62.6 us
  matrix products: 17.5 us -> 12.2 us
    all_to_all x2 -> x0, blocking collectives: 119 us -> none  [the longest x1 62.3 us: shards(): lax.all_to_all(outgoing_rows, 'req', split_axis=0, concat_axis=0, tiled=T...]
    psum x2 -> x0, waiting for transfers between devices: 83 us -> none  [the longest x1 42.1 us: shards(): attn_out = lax.psum(attn_part, 'tp')]
    pallas_call x0 -> x1, Pallas kernels: none -> 45.2 us  [moe_call(): pl.pallas_call(moe_kernel, out_shape=(jax.ShapeDtypeStruct((32, 1024), BF...]
    dot_general x5 -> x0, matrix products: 7.24 us -> none  [the longest x1 2.9 us: shards(): jnp.dot(combine, returned.reshape(buffer, -1), precision=lax.Precision.HI...]
    reshape x2 -> x1, local copies, waits for them, and re-layouts: 6.04 us -> 0.03 us  [shards(): flat_tokens = tokens_new.reshape(row_count, model_width)]
    unnamed x43 -> x39, local copies, waits for them, and re-layouts: 12.7 us -> 13.3 us
  transfers between devices with their start and end apart: 3 -> 1, of which waited for: 3 -> 1; matrix products, arithmetic and copies ran while one was open for 8% -> 17% of each run, Pallas kernels for 0% -> 0%
where the time goes in v1:
time: 214 us; the launch traced here: 212 us
  local copies, waits for them, and re-layouts  62.6 us (29%)
  waiting for transfers between devices  57.9 us (27%)
  Pallas kernels  45.2 us (21%)
  other arithmetic  19.2 us (9%)
  starting transfers between devices  13.4 us (6%)
  matrix products  12.2 us (6%)
    all_to_all x1, waiting for transfers between devices, shards(): lax.all_to_all(outgoing, 'req', split_axis=0, concat_axis=0, tiled=True)  57.9 us
    pallas_call x1, Pallas kernels, moe_call(): pl.pallas_call(moe_kernel, out_shape=(jax.ShapeDtypeStruct((32, 1024), BF...  45.2 us
    all_to_all x1, starting transfers between devices, shards(): lax.all_to_all(outgoing, 'req', split_axis=0, concat_axis=0, tiled=True)  13.4 us
    unnamed x39, local copies, waits for them, and re-layouts  13.3 us
    reshape x1, local copies, waits for them, and re-layouts, shards(): arrived.reshape(req_count * slot_cap, page_size, 2, kv_heads, HEAD_DIM)  11.1 us
    all_to_all x1, local copies, waits for them, and re-layouts, shards(): lax.all_to_all(outgoing, 'req', split_axis=0, concat_axis=0, tiled=True)  10.9 us
    gather x1, local copies, waits for them, and re-layouts, shards(): jnp.take(slot_page_cache, slot_index, axis=0)  10.6 us
    select_n x2, other arithmetic, shards(): jnp.take(slot_page_cache, slot_index, axis=0)  7.9 us
  transfers between devices with their start and end apart: 1, of which 1 were waited for; matrix products, arithmetic and copies ran while one was open for 17% of the time, Pallas kernels for 0%

profile of v1, /device:TPU:1, one launch (start us, length us, event | category | flops | bytes accessed | tf_op | source)
XLA Modules:
  0.0 212.1 jit_solution(311032751647960765)
XLA Ops:
  0.6 0.0 copy-start
  0.7 0.9 reshape.405
  1.6 0.1 convert_reduce_fusion
  1.7 0.1 select_reduce_fusion
  1.8 0.4 copy-done
  2.2 10.6 %gather_fusion = bf16[64,128,2,128]{3,2,1,0:T(2,128)(2,1)} fusion(bf16[32,128,2,128]{3,2,1,0:T(2,128)(2,1)S(1)} %copy-done, s32[1024]{0:T(1024)S(1)} %pad_clamp_fusion), kind=kCustom, calls=%fused_computation | custom fusion | bytes 8388864 | tf_op jit(solution)/shard_map/jit(_take)/gather | solution.py:405
  12.9 7.9 %fusion.4 = bf16[64,1,128,2,128]{4,3,2,1,0:T(2,128)(2,1)} fusion(bf16[64,128,2,128]{3,2,1,0:T(2,128)(2,1)} %gather_fusion, pred[64]{0:T(512)(128)(4,1)S(1)} %compare_and_fusion), kind=kLoop, calls=%fused_computation.9 | loop fusion | flops 2097152 | bytes 8388672 | tf_op jit(solution)/shard_map/jit(_take)/select_n | solution.py:405
  20.8 13.4 %all-to-all-start = ((bf16[64,1,128,2,128]{4,3,2,1,0:T(2,128)(2,1)}), bf16[64,1,128,2,128]{4,3,2,1,0:T(2,128)(2,1)}, u32[]{:S(2)}, u32[]{:S(2)}) async-start(bf16[64,1,128,2,128]{4,3,2,1,0:T(2,128)(2,1)} %fusion.4), calls=%async_computation | async-start | bytes 8388608 | tf_op jit(solution)/shard_map/all_to_all | solution.py:408
  34.2 0.6 dynamic-slice.5
  34.8 0.2 copy.230
  35.0 0.8 reduce_window_sum.11
  35.8 0.7 eq.92
  36.5 0.7 broadcast_in_dim_reshape.10
  37.2 11.1 %copy.234 = bf16[1,16,512,2,128]{2,4,3,1,0:T(8,128)(2,1)} copy(bf16[1,16,512,2,128]{4,3,2,1,0:T(2,128)(2,1)} %param.22) | data formatting | bytes 8388608 | tf_op args[6]
  48.3 6.9 %reshape_squeeze.3 = bf16[16,4,128,2,2,64]{2,1,5,4,3,0:T(4,128)(2,1)} reshape(bf16[1,16,512,2,128]{2,4,3,1,0:T(8,128)(2,1)} %copy.234) | data formatting | bytes 8388608 | tf_op jit(solution)/shard_map/reshape;squeeze | solution.py:431
  56.0 0.1 fusion.20
  56.1 0.1 multiply_cosine_fusion
  56.3 0.8 fusion.51
  57.1 0.3 fusion.29
  57.4 0.1 subtract_convert_fusion
  57.5 0.1 fusion.63
  57.6 0.1 broadcast_compare_fusion
  57.7 0.0 copy-start.9
  57.7 4.3 %fusion.56 = (bf16[16,4,128,1,2,64]{2,1,5,4,3,0:T(4,128)(2,1)S(1)}, bf16[16,4,128,1,2,64]{2,1,5,4,3,0:T(4,128)(2,1)}) fusion(bf16[16,4,128,2,2,64]{2,1,5,4,3,0:T(4,128)(2,1)} %reshape_squeeze.3), kind=kLoop, calls=%fused_computation.115 | loop fusion | bytes 8388608 | tf_op jit(solution)/shard_map/slice | solution.py:438
  62.1 0.7 fusion.18
  62.7 1.5 fusion.52
  64.2 0.7 copy.237
  64.9 0.1 copy.362
  65.0 0.2 copy.238
  65.2 1.2 fusion.27
  66.4 0.8 subtract_convert_fusion.1
  67.2 0.1 maximum_bitcast_fusion
  67.3 0.1 pad_maximum_fusion
  67.4 0.7 fusion.36
  68.0 0.2 copy.242
  68.2 0.1 fusion.43
  68.3 0.1 fusion.54
  68.4 0.1 copy.258
  68.5 0.8 copy.265
  69.3 0.9 select_reduce_fusion.1
  70.2 0.1 reduce_or.9
  70.4 0.1 fusion.34
  70.5 0.2 fusion.40
  70.6 57.9 %all-to-all-done = bf16[64,1,128,2,128]{4,3,2,1,0:T(2,128)(2,1)} async-done(((bf16[64,1,128,2,128]{4,3,2,1,0:T(2,128)(2,1)}), bf16[64,1,128,2,128]{4,3,2,1,0:T(2,128)(2,1)}, u32[]{:S(2)}, u32[]{:S(2)}) %all-to-all-start) | async-done | bytes 4194336 | tf_op jit(solution)/shard_map/all_to_all | solution.py:408
  128.6 10.9 %copy.226 = bf16[64,1,128,2,128]{2,4,3,0,1:T(8,128)(2,1)} copy(bf16[64,1,128,2,128]{4,3,2,1,0:T(2,128)(2,1)} %all-to-all-done) | data formatting | bytes 8388608 | tf_op jit(solution)/shard_map/all_to_all | solution.py:408
  139.5 3.1 %fusion.6 = (f32[64,16,2,2,2]{1,4,2,0,3:T(2,128)S(1)}, f32[2,64,128,16,2,2]{2,3,5,4,1,0:T(8,128)S(1)}) fusion(pred[64,128]{1,0:T(8,128)(4,1)S(1)} %fusion.34, bf16[16,2,2,2,64]{4,0,3,2,1:T(8,128)(2,1)S(1)} %pad_maximum_fusion, bf16[64,128,2,2,64]{1,4,3,2,0:T(8,128)(2,1)} %bitcast.172), kind=kOutput, calls=%fused_computation.11 | convolution fusion | flops 137355264 | bytes 6348800 | tf_op jit(solution)/shard_map/sikgd,btkd->bsikgt/dot_general | solution.py:419
  142.6 4.4 %fusion.7 = (f32[64,16,2,2,2]{1,4,2,0,3:T(2,128)S(1)}, f32[16,2,2,2]{0,3,1,2:T(2,128)S(1)}, bf16[64,16,2,2,2,128]{5,1,4,2,0,3:T(8,128)(2,1)}) fusion(f32[2,64,128,16,2,2]{2,3,5,4,1,0:T(8,128)S(1)} %get-tuple-element.73, f32[64,16,2,2,2]{1,4,2,0,3:T(2,128)S(1)} %get-tuple-element.72, pred[64,128]{1,0:T(8,128)(4,1)S(1)} %fusion.34), kind=kLoop, calls=%fused_computation.12 | loop fusion | flops 8380288 | bytes 6365696 | tf_op jit(solution)/shard_map/reduce_sum | solution.py:44
  147.0 0.1 copy.248
  147.1 0.3 multiply_reduce_fusion
  147.4 0.2 multiply_reduce_fusion.1
  147.6 0.1 copy.260
  147.7 0.1 copy.249
  147.8 11.1 %copy.288 = bf16[64,1,128,2,128]{2,4,0,3,1:T(8,128)(2,1)} copy(bf16[64,1,128,2,128]{4,3,2,1,0:T(2,128)(2,1)} %all-to-all-done) | data formatting | bytes 8388608 | tf_op jit(solution)/shard_map/reshape | solution.py:417
  158.9 3.6 %fusion = f32[16,2,2,2,64]{4,0,3,1,2:T(8,128)S(1)} fusion(bf16[64,128,2,2,64]{1,4,3,0,2:T(8,128)(2,1)} %bitcast.171, bf16[64,16,2,2,2,128]{5,1,4,2,0,3:T(8,128)(2,1)} %get-tuple-element.58, f32[64,16,2,2,2]{1,4,2,0,3:T(2,128)S(1)} %get-tuple-element.53), kind=kOutput, calls=%fused_computation.3 | convolution fusion | flops 135258112 | bytes 4259840 | tf_op jit(solution)/shard_map/bsikgt,btkd->bsikgd/dot_general | solution.py:427
  162.5 0.0 copy-start.1
  162.6 1.2 fusion.17
  163.8 0.1 fusion.26
  164.0 0.1 reshape.408
  164.1 1.2 fusion.57.part_ref
  165.4 45.2 %shard_map.167 = (bf16[32,1024]{1,0:T(8,128)(2,1)S(1)}, f32[32,1]{1,0:T(8,128)S(1)}) custom-call(bf16[32,1024]{1,0:T(8,128)(2,1)S(1)} %reshape.404.tok_ref, f32[32,1024]{1,0:T(8,128)S(1)} %fusion.57.part_ref, s32[32,8]{1,0:T(8,128)S(1)} %bitcast.167, f32[3,1024]{1,0:T(4,128)S(1)} %copy-done.4, bf16[32,1024]{1,0:T(8,128)(2,1)S(1)} %bitcast.168, ...), custom_call_target="tpu_custom_call" | custom-call | tf_op jit(solution)/shard_map/pallas_call | solution.py:322
  210.6 0.7 reshape.411
  211.3 0.1 reduce.6
  211.4 0.1 reshape.412
  211.5 0.7 copy.266
  (53 shorter events, 0.3 us)
Async XLA Ops:
  0.6 1.6 copy-start
  20.8 13.4 %copy-start.16 = (s32[64]{0:T(128)S(1)}, s32[64]{0:T(128)}, u32[]{:S(2)}) copy-start(s32[64]{0:T(128)} %param.17) | copy-start | bytes 772
  20.8 14.0 %copy-start.8 = (bf16[1024,256]{1,0:T(8,128)(2,1)S(1)}, bf16[1024,256]{1,0:T(8,128)(2,1)}, u32[]{:S(2)}) copy-start(bf16[1024,256]{1,0:T(8,128)(2,1)} %param.25) | copy-start | bytes 1572868
  20.8 15.0 %copy-start.12 = (s32[2048]{0:T(1024)S(1)}, s32[2048]{0:T(1024)}, u32[]{:S(2)}) copy-start(s32[2048]{0:T(1024)} %param.19) | copy-start | bytes 24580
  20.8 15.7 %copy-start.14 = (s32[2048]{0:T(1024)S(1)}, s32[2048]{0:T(1024)}, u32[]{:S(2)}) copy-start(s32[2048]{0:T(1024)} %param.20) | copy-start | bytes 24580
  20.8 107.8 %all-to-all-start = ((bf16[64,1,128,2,128]{4,3,2,1,0:T(2,128)(2,1)}), bf16[64,1,128,2,128]{4,3,2,1,0:T(2,128)(2,1)}, u32[]{:S(2)}, u32[]{:S(2)}) async-start(bf16[64,1,128,2,128]{4,3,2,1,0:T(2,128)(2,1)} %fusion.4), calls=%async_computation | async-start | bytes 8388608 | tf_op jit(solution)/shard_map/all_to_all | solution.py:408
  48.3 7.0 %copy-start.7 = (bf16[1,16,2,1024]{3,2,1,0:T(2,128)(2,1)S(1)}, bf16[1,16,2,1024]{3,2,1,0:T(2,128)(2,1)}, u32[]{:S(2)}) copy-start(bf16[1,16,2,1024]{3,2,1,0:T(2,128)(2,1)} %param.16) | copy-start | bytes 196612
  48.3 7.8 %copy-start.15 = (s32[1,16]{1,0:T(1,128)S(1)}, s32[1,16]{1,0:T(1,128)}, u32[]{:S(2)}) copy-start(s32[1,16]{1,0:T(1,128)} %param.18) | copy-start | bytes 196
  48.3 8.0 %slice-start = ((f32[3,1024]{1,0:T(4,128)}), f32[1,1024]{1,0:T(1,128)S(1)}, s32[]{:S(2)}) async-start(f32[3,1024]{1,0:T(4,128)} %gains_ref.1), calls=%async_computation.1 | async-start | bytes 8192 | tf_op jit(solution)/shard_map/slice | solution.py:370
  56.3 5.8 %copy-start.10 = (f32[16,2,32]{2,0,1:T(8,128)}, f32[16,2,32]{2,0,1:T(8,128)S(1)}, u32[]{:S(2)}) copy-start(f32[16,2,32]{2,0,1:T(8,128)S(1)} %get-tuple-element.69) | copy-start | bytes 12292
  57.7 7.2 %copy-start.9 = (bf16[1024,2,128]{2,1,0:T(2,128)(2,1)S(1)}, bf16[1024,2,128]{2,1,0:T(2,128)(2,1)}, u32[]{:S(2)}) copy-start(bf16[1024,2,128]{2,1,0:T(2,128)(2,1)} %param.26) | copy-start | bytes 1572868
  142.6 4.4 %copy-start.13 = (f32[16,2,2,2]{0,3,1,2:T(2,128)S(1)}, f32[16,2,2,2]{0,3,1,2:T(2,128)}, u32[]{:S(2)}) copy-start(f32[16,2,2,2]{0,3,1,2:T(2,128)} %copy.237) | copy-start | bytes 1540
  158.9 3.6 %copy-start.6 = (bf16[16,4,128,1,2,64]{2,1,5,4,3,0:T(4,128)(2,1)S(1)}, bf16[16,4,128,1,2,64]{2,1,5,4,3,0:T(4,128)(2,1)}, u32[]{:S(2)}) copy-start(bf16[16,4,128,1,2,64]{2,1,5,4,3,0:T(4,128)(2,1)} %get-tuple-element.60) | copy-start | bytes 6291460
  158.9 3.6 %copy-start.11 = (bf16[16,4,2,2,2,128]{5,4,1,2,3,0:T(2,128)(2,1)S(1)}, bf16[16,4,2,2,2,128]{5,4,1,2,3,0:T(2,128)(2,1)}, u32[]{:S(2)}) copy-start(bf16[16,4,2,2,2,128]{5,4,1,2,3,0:T(2,128)(2,1)} %get-tuple-element.61) | copy-start | bytes 393220
  162.5 2.8 %copy-start.1 = (bf16[1,1024,2,128]{3,2,1,0:T(2,128)(2,1)S(1)}, bf16[1,1024,2,128]{3,2,1,0:T(2,128)(2,1)}, u32[]{:S(2)}) copy-start(bf16[1,1024,2,128]{3,2,1,0:T(2,128)(2,1)} %param.29) | copy-start | bytes 1572868
  162.5 2.8 %copy-start.2 = (bf16[1,128,1024]{2,1,0:T(8,128)(2,1)S(1)}, bf16[1,128,1024]{2,1,0:T(8,128)(2,1)}, u32[]{:S(2)}) copy-start(bf16[1,128,1024]{2,1,0:T(8,128)(2,1)} %param.30) | copy-start | bytes 786436
  162.5 2.8 %copy-start.3 = (bf16[1024,32]{0,1:T(8,128)(2,1)S(1)}, bf16[1024,32]{0,1:T(8,128)(2,1)}, u32[]{:S(2)}) copy-start(bf16[1024,32]{0,1:T(8,128)(2,1)} %param.28) | copy-start | bytes 196612
  162.6 2.8 %copy-start.4 = (f32[3,1024]{1,0:T(4,128)S(1)}, f32[3,1024]{1,0:T(4,128)}, u32[]{:S(2)}) copy-start(f32[3,1024]{1,0:T(4,128)} %gains_ref.1) | copy-start | bytes 36868
  162.6 2.8 %copy-start.5 = (f32[1024]{0:T(1024)S(1)}, f32[1024]{0:T(1024)}, u32[]{:S(2)}) copy-start(f32[1024]{0:T(1024)} %param.31) | copy-start | bytes 12292

commit v2 on v1

--- a/solution.py
+++ b/solution.py
@@ -5,45 +5,9 @@
 from jax.experimental.pallas import tpu as pltpu
 from jax.sharding import PartitionSpec as P
 
-HEAD_DIM = 64
-MOST = 12
-
-
 EPSILON = 1e-05
 ROPE_BASE = 10000.0
 LOWEST = -1e30
-
-
-def rms_scale(values, gain_row):
-    widened = values.astype(jnp.float32)
-    return (
-        widened
-        * lax.rsqrt(jnp.mean(widened * widened, axis=-1, keepdims=True) + EPSILON)
-        * gain_row
-    )
-
-
-def apply_rotary(vectors, token_positions):
-    half_width = vectors.shape[-1] // 2
-    frequency = ROPE_BASE ** (-jnp.arange(half_width, dtype=jnp.float32) / half_width)
-    angles = token_positions.astype(jnp.float32)[..., None] * frequency
-    cosine = jnp.cos(angles)[..., None, :]
-    sine_part = jnp.sin(angles)[..., None, :]
-    leading = vectors[..., :half_width]
-    trailing = vectors[..., half_width:]
-    return jnp.concatenate(
-        [leading * cosine - trailing * sine_part, trailing * cosine + leading * sine_part], axis=-1
-    )
-
-
-def block_stats(scores, visible):
-    block_top = jnp.max(jnp.where(visible, scores, LOWEST), axis=-1)
-    weights = jnp.where(
-        visible, jnp.exp(jnp.where(visible, scores - block_top[..., None], 0.0)), 0.0
-    )
-    return (block_top, jnp.sum(weights, axis=-1), weights.astype(jnp.bfloat16))
-
-
 MESH = pl.DeviceIdType.MESH
 F32 = jnp.float32
 BF16 = jnp.bfloat16
@@ -291,204 +255,468 @@
     ]
 
 
-def moe_kernel(tok_ref, part_ref, routes_ref, gains_ref, router_ref, ein_ref, eout_ref, score_ref,
-               out_ref, row_score_ref, attn_slots, asend, arecv, win, *rest):
+def rotate(values, cosine, sine):
+    width = values.shape[1]
+    first = iota((1, width), 1) % 64 < 32
+    partner = jnp.where(first, pltpu.roll(values, width - 32, 1), pltpu.roll(values, 32, 1))
+    return values * cosine + partner * sine
+
+
+def masked_softmax(scores, visible):
+    top = jnp.max(jnp.where(visible, scores, LOWEST), axis=-1, keepdims=True)
+    weights = jnp.where(visible, jnp.exp(jnp.where(visible, scores - top, 0.0)), 0.0)
+    return top, jnp.sum(weights, axis=-1, keepdims=True), weights
+
+
+def shift_lanes(weights):
+    parts = [
+        pltpu.roll(weights[:, at : at + 128], 1, 1) for at in range(0, weights.shape[1], 128)
+    ]
+    return jnp.concatenate(parts, axis=1).astype(BF16)
+
+
+def as_row(column):
+    square = iota((128, 128), 0) == iota((128, 128), 1)
+    return jnp.sum(jnp.where(square, column, 0.0), axis=0, keepdims=True)
+
+
+def z_order(k):
+    return (k + 1) // 2 if k % 2 else (8 - k // 2) % 8
+
+
+def merge_weights(stats):
+    top = stats[0][0]
+    for other, _ in stats[1:]:
+        top = jnp.maximum(top, other)
+    shares = [jnp.exp(part - top) * total for part, total in stats]
+    total = shares[0]
+    for share in shares[1:]:
+        total = total + share
+    scale = 1.0 / jnp.maximum(total, 1e-30)
+    return top, total, [share * scale for share in shares]
+
+
+def widen(columns, at):
+    return jnp.where(iota((64, 128), 1) < 64, columns[:64, at : at + 1], columns[64:, at : at + 1])
+
+
+def three_parts(values):
+    high = values.astype(BF16)
+    rest = values - high.astype(F32)
+    middle = rest.astype(BF16)
+    return high, middle, (rest - middle.astype(F32)).astype(BF16)
+
+
+def query_sends(req, tp, q_all, qz_s, qz_r):
+    z, x, c = req // 8, req % 8 // 2, req % 2
+    for dz in (4, 3, 5, 2, 6, 1, 7):
+        remote(
+            q_all.at[z, x, c], q_all.at[z, x, c], qz_s.at[dz], qz_r.at[z],
+            (z + dz) % 8 * 8 + x * 2 + c, tp,
+        ).start()
+
+
+def query_forward_x(req, tp, q_all, qz_r, qx_s, qx_r, qc_s, qc_r):
+    z, x, c = req // 8, req % 8 // 2, req % 2
+    for k in range(8):
+        zz = (z + z_order(k)) % 8
+        if k:
+            remote(
+                q_all.at[z, x, c], q_all.at[zz, x, c], qx_s.at[0, 0], qz_r.at[zz], req, tp
+            ).wait_recv()
+        for dx in (2, 1, 3):
+            remote(
+                q_all.at[zz, x, c], q_all.at[zz, x, c], qx_s.at[zz, dx], qx_r.at[zz, x],
+                z * 8 + (x + dx) % 4 * 2 + c, tp,
+            ).start()
+        remote(
+            q_all.at[zz, x, c], q_all.at[zz, x, c], qc_s.at[zz, x], qc_r.at[zz, x],
+            z * 8 + x * 2 + 1 - c, tp,
+        ).start()
+
+
+def query_forward_core(req, tp, q_all, qx_s, qx_r, qc_s, qc_r):
+    z, x, c = req // 8, req % 8 // 2, req % 2
+    for k in range(8):
+        zz = (z + z_order(k)) % 8
+        for dx in (1, 3, 2):
+            xx = (x + dx) % 4
+            remote(
+                q_all.at[z, x, c], q_all.at[zz, xx, c], qx_s.at[0, 0], qx_r.at[zz, xx], req, tp
+            ).wait_recv()
+            remote(
+                q_all.at[zz, xx, c], q_all.at[zz, xx, c], qc_s.at[zz, xx], qc_r.at[zz, xx],
+                z * 8 + x * 2 + 1 - c, tp,
+            ).start()
+
+
+def query_finish(req, tp, q_all, qz_s, qx_s, qc_s, qc_r):
+    z, x, c = req // 8, req % 8 // 2, req % 2
+
+    @pl.loop(0, 32)
+    def _(i):
+        remote(
+            q_all.at[z, x, c], q_all.at[i // 4, i % 4, 1 - c], qx_s.at[0, 0],
+            qc_r.at[i // 4, i % 4], req, tp,
+        ).wait_recv()
+
+
+def query_drain(req, tp, q_all, qz_s, qx_s, qc_s):
+    z, x, c = req // 8, req % 8 // 2, req % 2
+
+    def drain(sem):
+        remote(q_all.at[z, x, c], q_all.at[z, x, c], sem, sem, req, tp).wait_send()
+
+    @pl.loop(1, 8)
+    def _(i):
+        drain(qz_s.at[i])
+
+    @pl.loop(0, 32)
+    def _(i):
+        drain(qc_s.at[i // 4, i % 4])
+
+    @pl.loop(0, 24)
+    def _(i):
+        drain(qx_s.at[i // 3, 1 + i % 3])
+
+
+def page_partials(meta, q_flat, pages, slot_out, slot_stats):
+    lane = iota((128, 256), 1)
+    even = lane % 2 == 0
+    left = iota((64, 128), 1) < 64
+
+    def one(v):
+        query = q_flat[meta[v]].astype(F32)
+        split = jnp.concatenate(
+            [jnp.where(left, query, 0.0), jnp.where(left, 0.0, query)], axis=0
+        ).astype(BF16)
+        rows = pages[v]
+        top, total, weights = masked_softmax(
+            mm_t(split, rows), even & (lane < 2 * meta[32 + v])
+        )
+        numer = mm(shift_lanes(weights), rows) / jnp.maximum(total, 1e-30)
+        slot_out[v] = jnp.where(left, numer[:64], numer[64:]).astype(BF16)
+        slot_stats[v] = jnp.concatenate([as_row(top), as_row(total)], axis=1)
+
+    @pl.loop(0, 8)
+    def _(step):
+        for at in range(4):
+            one(step * 4 + at)
+
+
+def partial_exchange(req, tp, meta, slot_out, slot_stats, send_o, send_s, ex_o, ex_s,
+                     es, er, lsem):
+    z, xc = req // 8, req % 8
+    empty = jnp.where(iota((1, 256), 1) < 128, LOWEST, 0.0)
+
+    def fill(other):
+        @pl.loop(0, 8)
+        def _(zz):
+            slot = meta[64 + zz * 8 + other]
+            held = jnp.maximum(slot, 0)
+            send_o[other, zz] = slot_out[held]
+            send_s[other, pl.ds(zz, 1), :] = jnp.where(slot >= 0, slot_stats[held], empty)
+
+    for step in (4, 5, 3, 2, 6, 7, 1):
+        other = (xc + step) % 8
+        fill(other)
+        remote(send_o.at[other], ex_o.at[xc], es.at[0, step], er.at[0, xc], z * 8 + other, tp).start()
+        remote(send_s.at[other], ex_s.at[xc], es.at[1, step], er.at[1, xc], z * 8 + other, tp).start()
+    fill(xc)
+    pltpu.make_async_copy(send_o.at[xc], ex_o.at[xc], lsem.at[0]).start()
+    pltpu.make_async_copy(send_s.at[xc], ex_s.at[xc], lsem.at[1]).start()
+
+
+def partial_merge(req, tp, send_o, send_s, ex_o, ex_s, comb_o, comb_s, ex2_o, ex2_s,
+                  er, es, lsem, fs, fr):
+    z, xc = req // 8, req % 8
+    pltpu.make_async_copy(send_o.at[xc], ex_o.at[xc], lsem.at[0]).wait()
+    pltpu.make_async_copy(send_s.at[xc], ex_s.at[xc], lsem.at[1]).wait()
+
+    @pl.loop(1, 8)
+    def _(step):
+        other = (xc + step) % 8
+        remote(send_o.at[0], ex_o.at[other], es.at[0, 0], er.at[0, other], req, tp).wait_recv()
+        remote(send_s.at[0], ex_s.at[other], es.at[1, 0], er.at[1, other], req, tp).wait_recv()
+
+    stats = [(ex_s[src][:, :128], ex_s[src][:, 128:]) for src in range(8)]
+    top, total, shares = merge_weights(stats)
+    columns = jnp.concatenate(shares + [jnp.zeros((64, 128), F32)], axis=0).T
+    for zz in range(8):
+        merged = jnp.zeros((64, 128), F32)
+        for src in range(8):
+            merged = merged + ex_o[src, zz].astype(F32) * widen(columns, src * 8 + zz)
+        comb_o[zz] = merged.astype(BF16)
+        comb_s[zz, :, 0:128] = top[zz : zz + 1]
+        comb_s[zz, :, 128:256] = total[zz : zz + 1]
+    for dz in (4, 3, 5, 2, 6, 1, 7):
+        to_z = (z + dz) % 8
+        remote(comb_o.at[to_z], ex2_o.at[z], fs.at[0, dz], fr.at[0, z], to_z * 8 + xc, tp).start()
+        remote(comb_s.at[to_z], ex2_s.at[z], fs.at[1, dz], fr.at[1, z], to_z * 8 + xc, tp).start()
+    pltpu.make_async_copy(comb_o.at[z], ex2_o.at[z], lsem.at[2]).start()
+    pltpu.make_async_copy(comb_s.at[z], ex2_s.at[z], lsem.at[3]).start()
+
+
+def prefix_finish(req, tp, comb_o, comb_s, ex2_o, ex2_s, lsem, fs, fr):
+    z, xc = req // 8, req % 8
+    pltpu.make_async_copy(comb_o.at[z], ex2_o.at[z], lsem.at[2]).wait()
+    pltpu.make_async_copy(comb_s.at[z], ex2_s.at[z], lsem.at[3]).wait()
+
+    @pl.loop(1, 8)
+    def _(dz):
+        other = (z + dz) % 8
+        remote(comb_o.at[0], ex2_o.at[other], fs.at[0, 0], fr.at[0, other], req, tp).wait_recv()
+        remote(comb_s.at[0], ex2_s.at[other], fs.at[1, 0], fr.at[1, other], req, tp).wait_recv()
+
+    stats = [(ex2_s[src][:, :128], ex2_s[src][:, 128:]) for src in range(8)]
+    top, total, shares = merge_weights(stats)
+    columns = jnp.concatenate(shares + [top, total, jnp.zeros((118, 128), F32)], axis=0).T
+    merged = jnp.zeros((64, 128), F32)
+    for src in range(8):
+        merged = merged + ex2_o[src].astype(F32) * widen(columns, src)
+    return widen(columns, 8), widen(columns, 9), merged
+
+
+def partial_drain(req, tp, send_o, send_s, comb_o, comb_s, es, fs):
+    @pl.loop(1, 8)
+    def _(i):
+        remote(send_o.at[0], send_o.at[0], es.at[0, i], es.at[0, i], req, tp).wait_send()
+        remote(send_s.at[0], send_s.at[0], es.at[1, i], es.at[1, i], req, tp).wait_send()
+        remote(comb_o.at[0], comb_o.at[0], fs.at[0, i], fs.at[0, i], req, tp).wait_send()
+        remote(comb_s.at[0], comb_s.at[0], fs.at[1, i], fs.at[1, i], req, tp).wait_send()
+
+
+def sample_queries(query_pair):
+    token = (iota((128, 32), 0) // 4 == iota((128, 32), 1)).astype(BF16)
+    rows = mm(token, query_pair)
+    row = iota((128, 128), 0)
+    mine = jnp.where(row % 2 == 0, rows[:, :128], rows[:, 128:])
+    return jnp.where(iota((128, 128), 1) // 64 == row % 4 // 2, mine, 0.0)
+
+
+def tail_partials(meta, queries, tail, tail_num, tail_top, tail_total, begin, end):
+    lane = iota((8, 1024), 1)
+    even = lane % 2 == 0
+
+    def one(s):
+        rows = tail[s]
+        query = queries[pl.ds(pl.multiple_of(s * 8, 8), 8), :].astype(BF16)
+        top, total, weights = masked_softmax(
+            mm_t(query, rows), even & (lane < 2 * meta[128 + s])
+        )
+        at = pl.ds(pl.multiple_of(s * 8, 8), 8)
+        tail_num[at, :] = mm(shift_lanes(weights), rows)
+        tail_top[at, :] = jnp.broadcast_to(top, (8, 128))
+        tail_total[at, :] = jnp.broadcast_to(total, (8, 128))
+
+    @pl.loop(begin // 4, end // 4)
+    def _(step):
+        for at in range(4):
+            one(step * 4 + at)
+
+
+def own_finish(queries, key_rot, value_new, tail_num, tail_top, tail_total):
+    row, col = iota((128, 32), 0), iota((128, 32), 1)
+    visible = (row // 8 == col // 2) & (col % 2 <= row % 8 // 4)
+    top_f, total_f, weights = masked_softmax(mm_t(queries.astype(BF16), key_rot), visible)
+    numer_f = mm(weights.astype(BF16), value_new)
+    top = jnp.maximum(tail_top[...], top_f)
+    share_t = jnp.exp(tail_top[...] - top)
+    share_f = jnp.exp(top_f - top)
+    total = share_t * tail_total[...] + share_f * total_f
+    numer = (share_t * tail_num[...] + share_f * numer_f) / total
+    row = iota((128, 128), 0)
+    own = iota((128, 128), 1) // 64 == row % 4 // 2
+    pick_row, pick_col = iota((64, 128), 0), iota((64, 128), 1)
+    pick = (pick_col // 4 == pick_row % 32) & (pick_col % 2 == pick_row // 32)
+    pick = pick.astype(F32).astype(BF16)
+
+    def compact(values, cut):
+        parts = cut(jnp.where(own, values, 0.0))
+        out = mm(pick, parts[0])
+        for part in parts[1:]:
+            out = out + mm(pick, part)
+        return out
+
+    return compact(top, three_parts), compact(total, three_parts), compact(numer, spread_halves)
+
+
+def layer_kernel(
+    meta, tok_ref, cos_ref, sin_ref, routes_ref, gains_ref, router_ref, score_ref,
+    wq_hbm, wkv_hbm, wo_hbm, pages_hbm, tail_hbm, ein_hbm, eout_hbm,
+    out_ref, row_score_ref,
+    wq, wkv, wo, pages, tail, ein, eout, loads, wkv_flat, q_all, queries,
+    tail_num, tail_top, tail_total, slot_out, slot_stats, send_o, send_s, ex_o, ex_s,
+    comb_o, comb_s, ex2_o, ex2_s,
+    qz_s, qz_r, qx_s, qx_r, qc_s, qc_r, es, er, fs, fr, plsem,
+    attn_slots, asend, arecv, win, *rest
+):
     req = lax.axis_index("req")
     tp = lax.axis_index("tp")
-    z = req // 8
-    xc = req % 8
+    z, x, c = req // 8, req % 8 // 2, req % 2
     barrier = pltpu.get_barrier_semaphore()
     for step in (1, 2, 3):
         pl.semaphore_signal(barrier, 1, device_id=(req, (tp + step) % 4), device_id_type=MESH)
 
-    @pl.loop(1, 40)
+    @pl.loop(1, 64)
     def _(i):
-        other = ((z + 6 + (i // 8 + 2) % 5) % 8) * 8 + (xc + i) % 8
-        pl.semaphore_signal(barrier, 1, device_id=(other, tp), device_id_type=MESH)
-
-    attn_slots[tp] = part_ref[...].astype(BF16)
-    pl.semaphore_wait(barrier, 42)
+        pl.semaphore_signal(barrier, 1, device_id=((req + i) % 64, tp), device_id_type=MESH)
+
+    moves = [
+        pltpu.make_async_copy(src, dst, loads.at[i])
+        for i, (src, dst) in enumerate(
+            [(wq_hbm, wq), (wkv_hbm, wkv), (tail_hbm, tail), (pages_hbm, pages), (wo_hbm, wo),
+             (ein_hbm, ein), (eout_hbm, eout)]
+        )
+    ]
+    for move in moves:
+        move.start()
+
+    normed = rms(tok_ref[...].astype(F32), gains_ref[0:1, :]).astype(BF16)
+    cosine, sine = cos_ref[...], sin_ref[...]
+    moves[0].wait()
+    query = rotate(
+        mm(normed, wq[...]),
+        jnp.concatenate([cosine, cosine], axis=1),
+        jnp.concatenate([sine, sine], axis=1),
+    )
+    query = query.astype(BF16).astype(F32) * 0.125
+    left = iota((32, 128), 1) < 64
+    low, high = query[:, :128], query[:, 128:]
+    first = jnp.where(left, low, pltpu.roll(high, 64, 1))
+    second = jnp.where(left, pltpu.roll(low, 64, 1), high)
+    q_all[z, x, c] = jnp.concatenate([first, second], axis=0).astype(BF16)
+    pl.semaphore_wait(barrier, 66)
+    query_sends(req, tp, q_all, qz_s, qz_r)
+
+    moves[1].wait()
+    deinterleave(wkv, wkv_flat)
+    key_value = mm(normed, wkv_flat[...])
+    key_rot = rotate(key_value[:, :128], cosine, sine).astype(BF16)
+    value_new = key_value[:, 128:].astype(BF16)
+    queries[...] = sample_queries(jnp.concatenate([first, second], axis=1).astype(BF16))
+    moves[2].wait()
+
+    query_forward_x(req, tp, q_all, qz_r, qx_s, qx_r, qc_s, qc_r)
+    tail_partials(meta, queries, tail, tail_num, tail_top, tail_total, 0, 12)
+    query_forward_core(req, tp, q_all, qx_s, qx_r, qc_s, qc_r)
+    moves[3].wait()
+    query_finish(req, tp, q_all, qz_s, qx_s, qc_s, qc_r)
+
+    page_partials(meta, q_all.reshape(64, 64, 128), pages, slot_out, slot_stats)
+    partial_exchange(req, tp, meta, slot_out, slot_stats, send_o, send_s, ex_o, ex_s, es, er, plsem)
+    tail_partials(meta, queries, tail, tail_num, tail_top, tail_total, 12, 16)
+    own_top, own_total, own_numer = own_finish(
+        queries[...], key_rot, value_new, tail_num, tail_top, tail_total
+    )
+    moves[4].wait()
+    moves[5].wait()
+    moves[6].wait()
+    deinterleave(ein, win)
+    query_drain(req, tp, q_all, qz_s, qx_s, qc_s)
+    partial_merge(req, tp, send_o, send_s, ex_o, ex_s, comb_o, comb_s, ex2_o, ex2_s,
+                  er, es, plsem, fs, fr)
+    top, total, numer = prefix_finish(req, tp, comb_o, comb_s, ex2_o, ex2_s, plsem, fs, fr)
+    most = jnp.maximum(top, own_top)
+    share = jnp.exp(top - most) * total
+    own_share = jnp.exp(own_top - most) * own_total
+    attn = ((share * numer + own_share * own_numer) / (share + own_share)).astype(BF16)
+    out_weight = jnp.concatenate([wo[0:64], wo[128:192], wo[64:128], wo[192:256]], axis=0)
+    part = mm(jnp.concatenate([attn[:32], attn[32:]], axis=1), out_weight)
+    attn_slots[tp] = part.astype(BF16)
     exchange_start(attn_slots, asend, arecv, req, tp)
-    deinterleave(ein_ref, win)
+    partial_drain(req, tp, send_o, send_s, comb_o, comb_s, es, fs)
     attn_out = exchange_finish(attn_slots, asend, arecv, req, tp)
     residual = (tok_ref[...].astype(F32) + attn_out).astype(BF16)
-    moe_stage(req, tp, residual, routes_ref, gains_ref, router_ref, eout_ref, score_ref,
+    moe_stage(req, tp, residual, routes_ref, gains_ref, router_ref, eout, score_ref,
               out_ref, row_score_ref, win, *rest)
 
 
-def moe_call(flat_tokens, attn_part, routing, norm_gains, router, expert_in, expert_out, score_weight):
+def layer_call(meta, *arrays):
     dma = pltpu.SemaphoreType.DMA
     vmem = pl.BlockSpec(memory_space=pltpu.VMEM)
+    anywhere = pl.BlockSpec(memory_space=pl.ANY)
+    buffers = [
+        pltpu.VMEM((1024, 256), BF16),
+        pltpu.VMEM((2048, 128), BF16),
+        pltpu.VMEM((256, 1024), BF16),
+        pltpu.VMEM((32, 256, 128), BF16),
+        pltpu.VMEM((16, 1024, 128), BF16),
+        pltpu.VMEM((2048, 128), BF16),
+        pltpu.VMEM((128, 1024), BF16),
+        dma((7,)),
+        pltpu.VMEM((1024, 256), BF16),
+        pltpu.VMEM((8, 4, 2, 64, 128), BF16),
+        pltpu.VMEM((128, 128), F32),
+        pltpu.VMEM((128, 128), F32),
+        pltpu.VMEM((128, 128), F32),
+        pltpu.VMEM((128, 128), F32),
+        pltpu.VMEM((32, 64, 128), BF16),
+        pltpu.VMEM((32, 1, 256), F32),
+        pltpu.VMEM((8, 8, 64, 128), BF16),
+        pltpu.VMEM((8, 8, 256), F32),
+        pltpu.VMEM((8, 8, 64, 128), BF16),
+        pltpu.VMEM((8, 8, 256), F32),
+        pltpu.VMEM((8, 64, 128), BF16),
+        pltpu.VMEM((8, 1, 256), F32),
+        pltpu.VMEM((8, 64, 128), BF16),
+        pltpu.VMEM((8, 1, 256), F32),
+        dma((8,)),
+        dma((8,)),
+        dma((8, 4)),
+        dma((8, 4)),
+        dma((8, 4)),
+        dma((8, 4)),
+        dma((2, 8)),
+        dma((2, 8)),
+        dma((2, 8)),
+        dma((2, 8)),
+        dma((4,)),
+        pltpu.VMEM((4, 32, 1024), BF16),
+        dma((4,)),
+        dma((4,)),
+    ]
     return pl.pallas_call(
-        moe_kernel,
+        layer_kernel,
         out_shape=(
             jax.ShapeDtypeStruct((32, 1024), BF16),
             jax.ShapeDtypeStruct((32, 1), F32),
         ),
-        in_specs=[vmem] * 8,
+        in_specs=[pl.BlockSpec(memory_space=pltpu.SMEM)] + [vmem] * 7 + [anywhere] * 7,
         out_specs=(vmem, vmem),
-        scratch_shapes=[pltpu.VMEM((4, 32, 1024), BF16), dma((4,)), dma((4,))] + moe_scratch(),
+        scratch_shapes=buffers + moe_scratch(),
         compiler_params=pltpu.CompilerParams(
             collective_id=0, has_side_effects=True, vmem_limit_bytes=48 * 1024 * 1024
         ),
-    )(flat_tokens, attn_part, routing, norm_gains, router.T, expert_in.reshape(2048, 128),
-      expert_out[0], score_weight[None])
+    )(meta, *arrays)
 
 
 def shards(
-    tokens_new,
-    prefix_len,
-    tail_len,
-    pool_home,
-    pool_page,
-    slot_page_cache,
-    tail_cache,
-    routes,
-    norm_gains,
-    query_weight,
-    key_value_weight,
-    out_weight,
-    router,
-    expert_in,
-    expert_out,
+    tokens_new, prefix_len, tail_len, pool_home, pool_page, slot_page_cache, tail_cache, routes,
+    norm_gains, query_weight, key_value_weight, out_weight, router, expert_in, expert_out,
     score_weight,
 ):
-    device = lax.axis_index("req")
-    req_count = lax.axis_size("req")
-    samples = tokens_new.shape[1]
-    fresh_count = tokens_new.shape[2]
-    model_width = tokens_new.shape[3]
-    row_count = samples * fresh_count
-    head_count = query_weight.shape[1] // HEAD_DIM
-    kv_heads = key_value_weight.shape[2] // HEAD_DIM
-    query_group_width = head_count // kv_heads
-    pool_slots = slot_page_cache.shape[0]
-    page_size = slot_page_cache.shape[1]
-    slot_cap = max(1, pool_slots // req_count)
-    score_scale = HEAD_DIM ** (-0.5)
-    flat_tokens = tokens_new.reshape(row_count, model_width)
-    normalized_input = rms_scale(flat_tokens, norm_gains[0]).astype(jnp.bfloat16)
-    query_vectors = jnp.dot(
-        normalized_input, query_weight, preferred_element_type=jnp.float32
-    ).reshape(samples, fresh_count, head_count, HEAD_DIM)
-    key_value_rows = jnp.dot(
-        normalized_input,
-        key_value_weight.reshape(model_width, 2 * kv_heads * HEAD_DIM),
-        preferred_element_type=jnp.float32,
-    ).reshape(samples, fresh_count, 2, kv_heads, HEAD_DIM)
-    own_length = jnp.take(prefix_len, device)
-    token_positions = (
-        own_length + tail_len[0][:, None] + jnp.arange(fresh_count, dtype=jnp.int32)[None, :]
+    req = lax.axis_index("req")
+    home = lax.dynamic_slice(pool_home, (req * 32,), (32,))
+    page = lax.dynamic_slice(pool_page, (req * 32,), (32,))
+    held = home[None, :] == jnp.arange(64, dtype=jnp.int32)[:, None]
+    slot_of = jnp.sum(held * (jnp.arange(32, dtype=jnp.int32) + 1)[None, :], axis=1) - 1
+    lengths = jnp.sum(jnp.where(held, prefix_len[:, None], 0), axis=0)
+    meta = jnp.concatenate([home, lengths - page * 128, slot_of, tail_len[0]])
+
+    fresh = jnp.arange(2, dtype=jnp.int32)
+    positions = (prefix_len[req] + tail_len[0][:, None] + fresh[None, :]).reshape(32)
+    frequency = ROPE_BASE ** (-jnp.arange(32, dtype=jnp.float32) / 32)
+    angles = positions.astype(jnp.float32)[:, None] * jnp.tile(frequency, 4)[None, :]
+    sign = jnp.where(jnp.arange(128) % 64 < 32, -1.0, 1.0).astype(jnp.float32)
+    layer_out, row_score = layer_call(
+        meta, tokens_new.reshape(32, 1024), jnp.cos(angles), jnp.sin(angles) * sign,
+        routes.reshape(32, 8), norm_gains, router.T, score_weight[None],
+        query_weight, key_value_weight.reshape(2048, 128), out_weight,
+        slot_page_cache.reshape(32, 256, 128), tail_cache.reshape(16, 1024, 128),
+        expert_in.reshape(2048, 128), expert_out[0],
     )
-    rotated_query = (
-        apply_rotary(query_vectors, token_positions)
-        .astype(jnp.bfloat16)
-        .reshape(samples, fresh_count, kv_heads, query_group_width, HEAD_DIM)
-    )
-    key_rot = apply_rotary(key_value_rows[:, :, 0], token_positions).astype(jnp.bfloat16)
-    value_new = key_value_rows[:, :, 1].astype(jnp.bfloat16)
-    owner_homes = pool_home.reshape(req_count, pool_slots)
-    owner_pages = pool_page.reshape(req_count, pool_slots)
-    own_home = jnp.take(owner_homes, device, axis=0)
-    slot_range = jnp.arange(pool_slots, dtype=jnp.int32)
-    cap_range = jnp.arange(slot_cap, dtype=jnp.int32)
-    same_home = own_home[:, None] == own_home[None, :]
-    earlier = slot_range[:, None] <= slot_range[None, :]
-    slot_rank = jnp.sum((same_home & earlier).astype(jnp.int32), axis=0)
-    picked_slots = (
-        own_home[None, None, :] == jnp.arange(req_count, dtype=jnp.int32)[:, None, None]
-    ) & (slot_rank[None, None, :] == cap_range[None, :, None] + 1)
-    slot_index = jnp.sum(
-        picked_slots.astype(jnp.int32) * slot_range[None, None, :], axis=-1
-    ).reshape(-1)
-    page_range = jnp.arange(page_size, dtype=jnp.int32)
-    outgoing = jnp.take(slot_page_cache, slot_index, axis=0).reshape(
-        (req_count, slot_cap) + slot_page_cache.shape[1:]
-    )
-    arrived = lax.all_to_all(outgoing, "req", split_axis=0, concat_axis=0, tiled=True)
-    home_match = owner_homes == device
-    home_rank = jnp.cumsum(home_match.astype(jnp.int32), axis=1)
-    wanted = home_match[:, None, :] & (home_rank[:, None, :] == cap_range[None, :, None] + 1)
-    page_ids = jnp.where(
-        jnp.any(wanted, axis=-1),
-        jnp.sum(wanted.astype(jnp.int32) * owner_pages[:, None, :], axis=-1),
-        -1,
-    ).reshape(-1)
-    blocks = arrived.reshape(req_count * slot_cap, page_size, 2, kv_heads, HEAD_DIM)
-    page_scores = (
-        jnp.einsum(
-            "sikgd,btkd->bsikgt", rotated_query, blocks[:, :, 0], preferred_element_type=jnp.float32
-        )
-        * score_scale
-    )
-    page_spots = page_ids[:, None] * page_size + page_range[None, :]
-    page_seen = ((page_spots < own_length) & (page_ids[:, None] >= 0))[:, None, None, None, None, :]
-    page_top, page_total, page_weights = block_stats(page_scores, page_seen)
-    page_numer = jnp.einsum(
-        "bsikgt,btkd->bsikgd", page_weights, blocks[:, :, 1], preferred_element_type=jnp.float32
-    )
-    tail_count = tail_cache.shape[2]
-    tail_block_list = tail_cache[0].reshape(
-        samples, tail_count // page_size, page_size, 2, kv_heads, HEAD_DIM
-    )
-    tail_scores = (
-        jnp.einsum(
-            "sikgd,sbtkd->sbikgt",
-            rotated_query,
-            tail_block_list[:, :, :, 0],
-            preferred_element_type=jnp.float32,
-        )
-        * score_scale
-    )
-    tail_spots = jnp.arange(tail_count, dtype=jnp.int32).reshape(tail_count // page_size, page_size)
-    tail_seen = (tail_spots[None] < tail_len[0][:, None, None])[:, :, None, None, None, :]
-    tail_top, tail_total, tail_weights = block_stats(tail_scores, tail_seen)
-    tail_numer = jnp.einsum(
-        "sbikgt,sbtkd->sbikgd",
-        tail_weights,
-        tail_block_list[:, :, :, 1],
-        preferred_element_type=jnp.float32,
-    )
-    fresh_scores = (
-        jnp.einsum("sikgd,sjkd->sikgj", rotated_query, key_rot, preferred_element_type=jnp.float32)
-        * score_scale
-    )
-    fresh_range = jnp.arange(fresh_count, dtype=jnp.int32)
-    fresh_seen = (fresh_range[None, :] <= fresh_range[:, None])[None, :, None, None, :]
-    fresh_top, fresh_total, fresh_weights = block_stats(fresh_scores, fresh_seen)
-    fresh_numer = jnp.einsum(
-        "sikgj,sjkd->sikgd", fresh_weights, value_new, preferred_element_type=jnp.float32
-    )
-    overall = jnp.maximum(
-        jnp.maximum(jnp.max(page_top, axis=0), jnp.max(tail_top, axis=1)), fresh_top
-    )
-    page_factor = jnp.exp(page_top - overall[None])
-    tail_factor = jnp.exp(tail_top - overall[:, None])
-    fresh_factor = jnp.exp(fresh_top - overall)
-    denominator = (
-        jnp.sum(page_factor * page_total, axis=0)
-        + jnp.sum(tail_factor * tail_total, axis=1)
-        + fresh_factor * fresh_total
-    )
-    numerator = (
-        jnp.sum(page_factor[..., None] * page_numer, axis=0)
-        + jnp.sum(tail_factor[..., None] * tail_numer, axis=1)
-        + fresh_factor[..., None] * fresh_numer
-    )
-    attn_rows = (
-        (numerator / denominator[..., None])
-        .astype(jnp.bfloat16)
-        .reshape(row_count, head_count * HEAD_DIM)
-    )
-    attn_part = jnp.dot(attn_rows, out_weight, preferred_element_type=jnp.float32)
-    layer_out, row_score = moe_call(
-        flat_tokens, attn_part, routes.reshape(row_count, -1), norm_gains, router, expert_in,
-        expert_out, score_weight,
-    )
-    return (
-        layer_out.reshape(1, samples, fresh_count, model_width),
-        row_score.reshape(1, samples, fresh_count),
-    )
+    return layer_out.reshape(1, 16, 2, 1024), row_score.reshape(1, 16, 2)
 
 
 def solution(mesh):

time: 214 us -> 111 us (0.52)
  waiting for transfers between devices: 57.9 us -> 0 us
  local copies, waits for them, and re-layouts: 62.6 us -> 14.2 us
  Pallas kernels: 45.2 us -> 91.7 us
  other arithmetic: 19.2 us -> 4 us
  starting transfers between devices: 13.4 us -> 0 us
  matrix products: 12.2 us -> 0 us
    all_to_all x1 -> x0, waiting for transfers between devices: 57.9 us -> none  [shards(): lax.all_to_all(outgoing, 'req', split_axis=0, concat_axis=0, tiled=True)]
    pallas_call x1, Pallas kernels: 45.2 us -> 91.7 us  [layer_call(): pl.pallas_call(layer_kernel, out_shape=(jax.ShapeDtypeStruct((32, 1024),...]
    all_to_all x1 -> x0, starting transfers between devices: 13.4 us -> none  [shards(): lax.all_to_all(outgoing, 'req', split_axis=0, concat_axis=0, tiled=True)]
    dot_general x9 -> x0, matrix products: 12.2 us -> none  [the longest x1 3.61 us: shards(): jnp.einsum('bsikgt,btkd->bsikgd', page_weights, blocks[:, :, 1], preferre...]
    reshape x6 -> x3, local copies, waits for them, and re-layouts: 12.9 us -> 1.61 us  [the longest x1 0.87 us: shards(): tokens_new.reshape(32, 1024)]
    all_to_all x1 -> x0, local copies, waits for them, and re-layouts: 10.9 us -> none  [shards(): lax.all_to_all(outgoing, 'req', split_axis=0, concat_axis=0, tiled=True)]
    gather x1 -> x0, local copies, waits for them, and re-layouts: 10.6 us -> none  [shards(): jnp.take(slot_page_cache, slot_index, axis=0)]
    another operation x3 -> x1, local copies, waits for them, and re-layouts: 8.21 us -> 0.01 us  [shards(): jnp.tile(frequency, 4)[None, :]]
  transfers between devices with their start and end apart: 1 -> 0, of which waited for: 1 -> 0; matrix products, arithmetic and copies ran while one was open for 17% -> 0% of each run, Pallas kernels for 0% -> 0%
where the time goes in v2:
time: 111 us
  Pallas kernels  91.7 us (83%)
  local copies, waits for them, and re-layouts  14.2 us (13%)
  other arithmetic  4 us (4%)
    pallas_call x1, Pallas kernels, layer_call(): pl.pallas_call(layer_kernel, out_shape=(jax.ShapeDtypeStruct((32, 1024),...  91.7 us
    unnamed x20, local copies, waits for them, and re-layouts  10.4 us

profile of v2, /device:TPU:1, one launch (start us, length us, event | category | flops | bytes accessed | tf_op | source)
XLA Modules:
  0.0 110.5 jit_solution(7514073008241549178)
XLA Ops:
  0.6 1.2 %dynamic_slice.11 = s32[1]{0:T(128)} dynamic-slice(s32[64]{0:T(128)} %param.17, s32[]{:T(128)S(6)} %select_n.32), dynamic_slice_sizes={1} | dynamic-slice | bytes 12 | tf_op jit(solution)/shard_map/dynamic_slice | solution.py:708
  1.9 1.3 %broadcast_add_fusion = s32[16]{0:T(128)S(1)} fusion(s32[]{:T(128)} %bitcast.1, s32[1,16]{1,0:T(1,128)} %param.18), kind=kLoop, calls=%fused_computation.13 | loop fusion | flops 16 | bytes 132 | tf_op jit(solution)/shard_map/add | solution.py:708
  3.2 0.8 dynamic_slice.9
  4.0 0.9 select_reduce_fusion.1
  4.8 0.8 multiply_subtract_fusion
  5.6 0.7 pad_add_fusion.meta
  6.3 0.1 mul.47
  6.4 0.1 add_convert_fusion
  6.5 0.1 convert_element_type.12
  6.6 0.8 copy.22
  7.3 0.1 fusion
  7.5 0.9 reshape.74.tok_ref
  8.4 0.0 copy-start
  8.4 1.6 %copy-done = bf16[32,128,2,128]{3,2,1,0:T(2,128)(2,1)S(1)} copy-done((bf16[32,128,2,128]{3,2,1,0:T(2,128)(2,1)S(1)}, bf16[32,128,2,128]{3,2,1,0:T(2,128)(2,1)}, u32[]{:S(2)}) %copy-start) | copy-done | bytes 2097176
  10.0 0.0 copy-start.1
  10.0 1.0 copy-done.1
  11.0 0.0 copy-start.2
  11.0 1.0 copy-done.2
  12.0 0.0 copy-start.3
  12.0 1.0 copy-done.3
  13.1 0.0 copy-start.4
  13.1 1.0 copy-done.4
  14.1 0.0 copy-start.5
  14.1 0.9 copy-done.5
  15.1 0.0 copy-start.6
  15.1 0.8 copy-done.6
  15.9 0.0 copy-start.7
  15.9 0.7 copy-done.7
  16.6 0.0 copy-start.8
  16.6 0.7 copy-done.8
  17.3 91.7 %shard_map.167 = (bf16[32,1024]{1,0:T(8,128)(2,1)S(1)}, f32[32,1]{1,0:T(8,128)S(1)}) custom-call(s32[144]{0:T(256)S(1)} %pad_add_fusion.meta, bf16[32,1024]{1,0:T(8,128)(2,1)S(1)} %reshape.74.tok_ref, f32[32,128]{1,0:T(8,128)S(1)} %get-tuple-element.15.cos_ref, f32[32,128]{1,0:T(8,128)S(1)} %get-tuple-element.14.sin_ref, s32[32,8]{1,0:T(8,128)S(1)} %bitcast.16, ...), custom_call_target="tpu_custom_call" | custom-call | tf_op jit(solution)/shard_map/pallas_call | solution.py:679
  109.0 0.7 reshape.80
  109.7 0.1 reduce
  109.8 0.1 reshape.81
  109.9 0.7 copy.23
  (5 shorter events, 0.0 us)
Async XLA Ops:
  8.4 1.6 %copy-start = (bf16[32,128,2,128]{3,2,1,0:T(2,128)(2,1)S(1)}, bf16[32,128,2,128]{3,2,1,0:T(2,128)(2,1)}, u32[]{:S(2)}) copy-start(bf16[32,128,2,128]{3,2,1,0:T(2,128)(2,1)} %param.21) | copy-start | bytes 6291460
  10.0 1.0 copy-start.1
  11.0 1.0 copy-start.2
  12.0 1.0 copy-start.3
  13.1 1.0 copy-start.4
  14.1 0.9 copy-start.5
  15.1 0.8 copy-start.6
  15.9 0.7 copy-start.7
  16.6 0.7 copy-start.8
